TPU v7x, 256 devices: a whole 4x4x8 slice. The times are simulated.
256 devices in a mesh: file: 8 (over x, core), blk: 32 (over z, y).
Axes of the slice: x: 4, y: 4, z: 8, core: 2. Of those that a mesh axis runs over, the one named last changes fastest.
Arguments:
- ctx_keys: bfloat16 [32768, 256], P(('file', 'blk')), parts along dimension 0, may hold values from -4 to 4
- ctx_values: bfloat16 [32768, 256], P(('file', 'blk')), parts along dimension 0, may hold values from -6 to 6
- middle_queries: bfloat16 [32768, 1792], P(('file', 'blk')), parts along dimension 0, may hold values from -40 to 40
- span_keys: bfloat16 [32768, 256], P(('file', 'blk')), parts along dimension 0, may hold values from -6 to 6
- span_values: bfloat16 [32768, 256], P(('file', 'blk')), parts along dimension 0, may hold values from -6 to 6
- span_len: int32 [256], P(('file', 'blk')), parts along dimension 0, may hold values from 36 to 128, as said below
- commit_pos: int32 [256, 2, 16], P(('file', 'blk')), parts along dimension 0, may hold values from 4 to 127, as said below
- commit_emb: bfloat16 [256, 2, 16, 3584], P(('file', 'blk')), parts along dimension 0, may hold values from -6 to 6
- w_key: bfloat16 [3584, 256], replicated, may hold values from -0.09375 to 0.09375
- w_value: bfloat16 [3584, 256], replicated, may hold values from -0.09375 to 0.09375
Outputs:
- span_out: bfloat16 [2, 32768, 1792], P(None, ('file', 'blk')), parts along dimension 1
There are 8 independent parts, one for each index of `file`. A program takes and returns all parts, laid end to end along the dimension named above; an argument that names none is the same for every part. Nothing has to cross between parts.
Inputs may be any that keep to these rules, and one draw needn't show every extreme that they name: `span_len`: some device's span fills all 128 slots in every draw. `commit_pos`: each device commits exactly 16 slots a step; a device's committed slots are distinct over all steps and lie below that device's span length.
All inputs are finite; a program needn't handle non-finite values.
Results may differ from a plain program's by a relative error of at most 0.0067.
Values may be sent and summed in bfloat16 or wider, within the bound.
No kernel may reach another device: no remote copies, remote signals or barrier semaphores. Data moves between devices by JAX's collectives and lax.ppermute only.
A program may use at most 256 MiB of HBM per device.

v0:
```python
import functools
import math

import jax
import jax.numpy as jnp
from jax import lax
from jax.experimental import pallas as pl
from jax.experimental.pallas import tpu as pltpu
from jax.sharding import PartitionSpec as P

BF16 = jnp.bfloat16
F32 = jnp.float32
HEAD = 128
GROUPS = 2
PER_GROUP = 7
HEADS = GROUPS * PER_GROUP
COMMIT = 16
SLOTS = 128
COMMON = SLOTS - COMMIT
BOTH = SLOTS - 2 * COMMIT
KVW = GROUPS * HEAD
PAIR = 2 * KVW
ROWS = PER_GROUP * COMMON
MARK = 1e30
SCALE = math.log2(math.e) / math.sqrt(HEAD)
VMEM = pl.BlockSpec(memory_space=pltpu.VMEM)
SMEM = pl.BlockSpec(memory_space=pltpu.SMEM)


def vmem_params(mib):
    return pltpu.CompilerParams(vmem_limit_bytes=mib << 20)


def named_slots(pos_ref, step):
    slot = lax.broadcasted_iota(jnp.int32, (SLOTS, COMMIT), 0)
    return (slot == pos_ref[0, step : step + 1, :]).astype(F32)


def rank_of(flag):
    row = lax.broadcasted_iota(jnp.int32, (SLOTS, SLOTS), 0)
    col = lax.broadcasted_iota(jnp.int32, (SLOTS, SLOTS), 1)
    return jnp.dot((col < row).astype(BF16), flag.astype(BF16), preferred_element_type=F32)


def lanes():
    return lax.broadcasted_iota(jnp.int32, (SLOTS, SLOTS), 1).astype(F32)


def flag_of(named):
    return jnp.broadcast_to(jnp.max(named, axis=1, keepdims=True), (SLOTS, SLOTS))


def select_rows(chosen, rows):
    return lax.dot_general(
        chosen.astype(BF16), rows, (((0,), (0,)), ((), ())), preferred_element_type=F32
    ).astype(BF16)


def join_kernel(keys_ref, values_ref, out_ref, sems):
    copies = [
        pltpu.make_async_copy(keys_ref, out_ref.at[:, pl.ds(0, KVW)], sems.at[0]),
        pltpu.make_async_copy(values_ref, out_ref.at[:, pl.ds(KVW, KVW)], sems.at[1]),
    ]
    for copy in copies:
        copy.start()
    for copy in copies:
        copy.wait()


def prepare_kernel(len_ref, pos_ref, *refs):
    sources, out_ref, held, sems = refs[:5], refs[5], refs[6:11], refs[11]
    copies = [
        pltpu.make_async_copy(source, target, sems.at[i])
        for i, (source, target) in enumerate(zip(sources, held))
    ]
    for copy in copies:
        copy.start()
    emb_ref, wk_ref, wv_ref, sk_ref, sv_ref = held
    named0 = named_slots(pos_ref, 0)
    named1 = named_slots(pos_ref, 1)
    in0 = flag_of(named0)
    stay = 1.0 - flag_of(named1)
    chosen = jnp.where(rank_of(stay) == lanes(), stay, 0.0)
    dead = lax.broadcasted_iota(jnp.int32, (SLOTS, KVW), 0) >= len_ref[0]
    for part, (w_ref, s_ref) in enumerate(((wk_ref, sk_ref), (wv_ref, sv_ref))):
        if part == 0:
            copies[0].wait()
        copies[1 + part].wait()
        copies[3 + part].wait()
        emb = emb_ref[0].reshape(2 * COMMIT, emb_ref.shape[3])
        new = jnp.dot(emb, w_ref[...], preferred_element_type=F32).astype(BF16)
        put = jnp.dot(named0.astype(BF16), new[:COMMIT], preferred_element_type=F32)
        now = jnp.where(
            jnp.concatenate([in0, in0], axis=1) > 0.5, put, s_ref[...].astype(F32)
        )
        filler = now[0:1, :] if part == 0 else jnp.full((1, KVW), MARK, F32)
        now = jnp.where(dead, filler, now).astype(BF16)
        cols = slice(part * KVW, (part + 1) * KVW)
        out_ref[0:COMMON, cols] = select_rows(chosen, now)[:COMMON]
        out_ref[COMMON:SLOTS, cols] = select_rows(named1, now)
        out_ref[SLOTS : SLOTS + COMMIT, cols] = new[COMMIT:]


def query_order(pos_ref):
    in0 = flag_of(named_slots(pos_ref, 0))
    in1 = flag_of(named_slots(pos_ref, 1))
    never = (1.0 - in0) * (1.0 - in1)
    first = jnp.where(rank_of(never) == lanes(), never, 0.0)
    second = jnp.where(rank_of(in1) + float(BOTH) == lanes(), in1, 0.0)
    return first, second


def queries_kernel(pos_ref, mq_ref, out_ref):
    first, second = query_order(pos_ref)
    picked = select_rows(first + second, mq_ref[...])
    for head in range(HEADS):
        out_ref[head * COMMON : (head + 1) * COMMON, :] = picked[
            :COMMON, head * HEAD : (head + 1) * HEAD
        ]


def attend(q, keys, values, old_acc, old_max):
    scores = lax.dot_general(q, keys, (((1,), (1,)), ((), ())), preferred_element_type=F32)
    new_max = jnp.maximum(old_max, jnp.max(scores, axis=1, keepdims=True))
    weights = jnp.exp2((scores - new_max[:, :1]) * SCALE).astype(BF16)
    keep = jnp.exp2((old_max - new_max) * SCALE)
    gained = jnp.dot(weights, values, preferred_element_type=F32)
    return old_acc * jnp.concatenate([keep, keep], axis=1) + gained, new_max


def lane_block(index):
    return pl.ds(pl.multiple_of(index * HEAD, HEAD), HEAD)


def with_flags(values):
    marked = values > MARK / 2
    zero = jnp.zeros_like(values)
    return jnp.where(marked, zero, values), jnp.where(marked, zero, jnp.ones_like(values))


def gather_rows(refs, block, keys, values):
    at = 0
    for ref in refs:
        flat = len(ref.shape) == 2
        count = ref.shape[0] * (1 if flat else block)
        for index in range(2 * GROUPS):
            cols = slice(index * HEAD, (index + 1) * HEAD)
            if flat:
                got = ref[:, cols]
            else:
                got = ref[:, :block, cols].reshape(count, HEAD)
            rows = slice(at, at + count)
            if index < GROUPS:
                keys[rows, cols] = got
            else:
                first = 2 * (index - GROUPS) * HEAD
                value, flag = with_flags(got)
                values[rows, first : first + HEAD] = value
                values[rows, first + HEAD : first + 2 * HEAD] = flag
        at += count
    spare = keys.shape[0] - at
    if spare:
        keys[at:, :] = keys[:spare, :]
        values[at:, :] = jnp.zeros((spare, PAIR), BF16)


def value_block(group):
    return pl.ds(pl.multiple_of(group * 2 * HEAD, 2 * HEAD), 2 * HEAD)


def head_rows(group, head):
    return pl.ds(pl.multiple_of((group * PER_GROUP + head) * COMMON, COMMIT), COMMON)


TILES = ((0, 400), (400, 384))
LIMIT = 1e30


def gained(q_ref, keys, values, top, rows):
    scores = lax.dot_general(
        q_ref[rows, :], keys, (((1,), (1,)), ((), ())), preferred_element_type=F32
    )
    weights = jnp.exp2((scores - top[rows, :][:, :1]) * SCALE).astype(BF16)
    return jnp.dot(weights, values, preferred_element_type=F32)


def tile_rows(group, start, size):
    return pl.ds(pl.multiple_of(group * ROWS + start, COMMIT), size)


def too_large(total):
    return jnp.max(jnp.where(total < LIMIT, 0.0, 1.0)) > 0.5


def first_kernel(q_ref, piece, acc, top, keys, values):
    gather_rows([piece], COMMON, keys, values)

    def one_group(group, _):
        for head in range(PER_GROUP):
            rows = head_rows(group, head)
            acc[rows, :], top[rows, :] = attend(
                q_ref[rows, :],
                keys[:, lane_block(group)],
                values[:, value_block(group)],
                jnp.zeros((COMMON, 2 * HEAD), F32),
                jnp.full((COMMON, HEAD), -1e30, F32),
            )
        return 0

    lax.fori_loop(0, GROUPS, one_group, 0)


def piece_kernel(span, count, *refs):
    refs = list(refs)
    q_ref, acc_in, top_in = [refs.pop(0) for _ in range(3)]
    pieces = [refs.pop(0) for _ in range(count)]
    acc, top = refs.pop(0), refs.pop(0)
    old, new = (refs.pop(0), refs.pop(0)) if span else (None, None)
    keys, values = refs
    gather_rows(pieces, COMMON, keys, values)
    at = 0
    for piece in pieces if span else ():
        blocks = piece.shape[0]
        old[at : at + blocks] = piece[:, COMMON:SLOTS, :]
        new[at : at + blocks] = piece[:, SLOTS:, :]
        at += blocks

    def one_group(group, _):
        for start, size in TILES:
            rows = tile_rows(group, start, size)
            acc[rows, :] = acc_in[rows, :] + gained(
                q_ref, keys[:, lane_block(group)], values[:, value_block(group)], top_in, rows
            )
        return 0

    lax.fori_loop(0, GROUPS, one_group, 0)
    again = too_large(acc[:, HEAD:])
    top[...] = top_in[...]

    @pl.when(again)
    def _():
        def one_head(index, _):
            group = index // PER_GROUP
            rows = head_rows(0, index)
            acc[rows, :], top[rows, :] = attend(
                q_ref[rows, :],
                keys[:, lane_block(group)],
                values[:, value_block(group)],
                acc_in[rows, :],
                top_in[rows, :],
            )
            return 0

        lax.fori_loop(0, HEADS, one_head, 0)


def estimate(keys):
    work = HEADS * COMMON * keys
    return pl.CostEstimate(
        flops=8 * work * HEAD, bytes_accessed=keys * PAIR * 2, transcendentals=work
    )


STATE = (
    jax.ShapeDtypeStruct((HEADS * COMMON, 2 * HEAD), F32),
    jax.ShapeDtypeStruct((HEADS * COMMON, HEAD), F32),
)
ANY = pl.BlockSpec(memory_space=pltpu.HBM)


def padded(rows):
    return [
        pltpu.VMEM((pl.cdiv(rows, HEAD) * HEAD, width), BF16) for width in (KVW, PAIR)
    ]


def attend_first(queries, piece):
    return pl.pallas_call(
        first_kernel,
        out_shape=STATE,
        in_specs=[VMEM] * 2,
        out_specs=[VMEM] * 2,
        scratch_shapes=padded(piece.shape[0]),
        compiler_params=vmem_params(24),
        cost_estimate=estimate(piece.shape[0]),
        name="attend_first",
    )(queries, piece)


def attend_piece(name, queries, state, pieces, span=False):
    rows = sum(piece.shape[0] for piece in pieces) * (COMMON if span else 1)
    outs = list(STATE)
    if span:
        outs += [jax.ShapeDtypeStruct((rows // COMMON, COMMIT, PAIR), BF16)] * 2
    got = pl.pallas_call(
        functools.partial(piece_kernel, span, len(pieces)),
        out_shape=outs,
        in_specs=[VMEM] * (3 + len(pieces)),
        out_specs=[VMEM] * len(outs),
        scratch_shapes=padded(rows),
        compiler_params=vmem_params(24),
        cost_estimate=estimate(rows),
        name=name,
    )(queries, *state, *pieces)
    return tuple(got[:2]), got[2:]


def ratio(full):
    return (full[:, :HEAD] / full[:, HEAD:]).astype(BF16)


def last_kernel(count, extra_count, *refs):
    refs = list(refs)
    len_ref, pos_ref, q_ref, acc, top = [refs.pop(0) for _ in range(5)]
    sources = [[refs.pop(0) for _ in range(n)] for n in (count, extra_count, extra_count)]
    out_ref, rows_out, done, largest = [refs.pop(0) for _ in range(4)]
    held = [(refs.pop(0), refs.pop(0)) for _ in range(3)]
    for source, (keys, values) in zip(sources, held):
        gather_rows(source, COMMIT, keys, values)
    rows_out[:, COMMON:, :] = jnp.zeros((2, COMMIT, HEADS * HEAD), BF16)

    def one_group(group, _):
        for start, size in TILES:
            rows = tile_rows(group, start, size)
            adds = [
                gained(q_ref, keys[:, lane_block(group)], values[:, value_block(group)], top, rows)
                for keys, values in held
            ]
            common = acc[rows, :] + adds[0]
            for number in range(2):
                full = common + adds[1 + number]
                done[number, rows, :] = ratio(full)
                largest[number, rows, :] = full[:, HEAD:]
        return 0

    lax.fori_loop(0, GROUPS, one_group, 0)

    @pl.when(too_large(largest[...]))
    def _():
        def one_head(index, _):
            group = index // PER_GROUP
            rows = head_rows(0, index)
            state = acc[rows, :], top[rows, :]
            for number, (keys, values) in enumerate(held):
                full = attend(
                    q_ref[rows, :], keys[:, lane_block(group)], values[:, value_block(group)], *state
                )
                if number == 0:
                    state = full
                else:
                    done[number - 1, rows, :] = ratio(full[0])
            return 0

        lax.fori_loop(0, HEADS, one_head, 0)

    first, second = query_order(pos_ref)
    live = lax.broadcasted_iota(jnp.int32, (SLOTS, SLOTS), 0) < len_ref[0]
    for number in range(2):
        for head in range(HEADS):
            rows_out[number, :COMMON, head * HEAD : (head + 1) * HEAD] = done[
                number, head * COMMON : (head + 1) * COMMON, :
            ]
        place = jnp.where(live, first + second if number == 0 else first, 0.0).astype(BF16)
        out_ref[number] = jnp.dot(
            place, rows_out[number], preferred_element_type=F32
        ).astype(BF16)


def attend_last(span_len, commit_pos, queries, state, pieces, olds, news):
    extra = sum(part.shape[0] for part in olds) * COMMIT
    sizes = [sum(piece.shape[0] for piece in pieces), extra, extra]
    return pl.pallas_call(
        functools.partial(last_kernel, len(pieces), len(olds)),
        out_shape=jax.ShapeDtypeStruct((2, SLOTS, HEADS * HEAD), BF16),
        in_specs=[SMEM] + [VMEM] * (4 + len(pieces) + 2 * len(olds)),
        out_specs=VMEM,
        scratch_shapes=[
            pltpu.VMEM((2, SLOTS, HEADS * HEAD), BF16),
            pltpu.VMEM((2, HEADS * COMMON, HEAD), BF16),
            pltpu.VMEM((2, HEADS * COMMON, HEAD), F32),
        ]
        + [scratch for size in sizes for scratch in padded(size)],
        compiler_params=vmem_params(24),
        cost_estimate=estimate(sum(sizes)),
        name="attend_last",
    )(span_len, commit_pos, queries, *state, *pieces, *olds, *news)


def in_hbm(x):
    return pltpu.with_memory_space_constraint(x, pltpu.HBM)


NZ, NY = 8, 4


def exchange(x, partner):
    pairs = []
    for z in range(NZ):
        for y in range(NY):
            pz, py = partner(z, y)
            pairs.append((z * NY + y, pz % NZ * NY + py % NY))
    return lax.ppermute(x, "blk", pairs)


def side(i, odd):
    return i + 1 if i % 2 == odd else i - 1


def z_even(x):
    return exchange(x, lambda z, y: (side(z, 0), y))


def z_odd(x):
    return exchange(x, lambda z, y: (side(z, 1), y))


def y_even(x):
    return exchange(x, lambda z, y: (z, side(y, 0)))


def y_odd(x):
    return exchange(x, lambda z, y: (z, side(y, 1)))


def y_far(x):
    return exchange(x, lambda z, y: (z, y + 2))


def round_z(even, odd):
    return z_even(odd), z_odd(even)


def per_device(
    ctx_keys,
    ctx_values,
    middle_queries,
    span_keys,
    span_values,
    span_len,
    commit_pos,
    commit_emb,
    w_key,
    w_value,
):
    together = lax.optimization_barrier
    ctx = pl.pallas_call(
        join_kernel,
        out_shape=jax.ShapeDtypeStruct((SLOTS, PAIR), BF16),
        in_specs=[ANY, ANY],
        out_specs=VMEM,
        scratch_shapes=[pltpu.SemaphoreType.DMA((2,))],
        compiler_params=vmem_params(4),
        name="join",
    )(in_hbm(ctx_keys), in_hbm(ctx_values))
    near = [y_even(ctx), y_odd(ctx), y_far(ctx)]
    held = [in_hbm(x) for x in (commit_emb, w_key, w_value, span_keys, span_values)]
    span = pl.pallas_call(
        prepare_kernel,
        out_shape=jax.ShapeDtypeStruct((SLOTS + COMMIT, PAIR), BF16),
        in_specs=[SMEM, VMEM] + [ANY] * len(held),
        out_specs=VMEM,
        scratch_shapes=[pltpu.VMEM(x.shape, x.dtype) for x in held]
        + [pltpu.SemaphoreType.DMA((len(held),))],
        compiler_params=vmem_params(12),
        name="prepare",
    )(span_len, commit_pos, *held)
    queries = pl.pallas_call(
        queries_kernel,
        out_shape=jax.ShapeDtypeStruct((HEADS * COMMON, HEAD), BF16),
        in_specs=[VMEM, VMEM],
        out_specs=VMEM,
        compiler_params=vmem_params(24),
        name="queries",
    )(commit_pos, middle_queries)

    near1 = round_z(span, span)
    near2 = round_z(*near1)

    def blocks(x):
        return x.reshape(-1, SLOTS + COMMIT, PAIR)

    ctx4 = jnp.concatenate([ctx] + near)
    state = attend_first(queries, ctx4)
    *near2, state = together((*near2, state))
    near3 = round_z(*near2)
    far = z_even(near3[1])
    first = jnp.concatenate([span, *near1, *near2])
    second = jnp.concatenate([*near3, far])
    first_y = y_even(first), y_odd(first)
    ctx1 = round_z(ctx4, ctx4)
    *ctx1, state = together((*ctx1, state))
    ctx2 = round_z(*ctx1)
    state, _ = attend_piece("attend_ctx1", queries, state, ctx1)
    *first_y, state = together((*first_y, state))
    cut = 3 * (SLOTS + COMMIT)
    first_far = y_even(first_y[1][:cut]), y_odd(first_y[0][cut:])
    *ctx2, state = together((*ctx2, state))
    ctx3 = round_z(*ctx2)
    second_y = y_even(second), y_odd(second)
    state, extra1 = attend_piece(
        "attend_span1", queries, state, [blocks(x) for x in (first, *first_y)], True
    )
    state, _ = attend_piece("attend_ctx2", queries, state, ctx2)
    second_y, ctx3, state = together((second_y, ctx3, state))
    cut = SLOTS + COMMIT
    second_far = y_even(second_y[1][:cut]), y_odd(second_y[0][cut:])
    ends = [z_even(ctx3[1])]
    state, extra2 = attend_piece(
        "attend_span2", queries, state, [blocks(x) for x in (*first_far, second)], True
    )
    state, _ = attend_piece("attend_ctx3", queries, state, ctx3)
    state, extra3 = attend_piece(
        "attend_span3", queries, state, [blocks(x) for x in (*second_y, *second_far)], True
    )
    olds = [extra[0] for extra in (extra1, extra2, extra3)]
    news = [extra[1] for extra in (extra1, extra2, extra3)]
    return attend_last(span_len, commit_pos, queries, state, ends, olds, news)


def solution(mesh):
    both = ("file", "blk")
    in_specs = (
        P(both, None),
        P(both, None),
        P(both, None),
        P(both, None),
        P(both, None),
        P(both),
        P(both, None, None),
        P(both, None, None, None),
        P(),
        P(),
    )
    return jax.shard_map(
        per_device, mesh=mesh, in_specs=in_specs, out_specs=P(None, both, None), check_vma=False
    )
```

profile of v0, /device:TPU:4, one launch (start us, length us, event | category | flops | bytes accessed | tf_op | source)
XLA Modules:
  0.0 94.8 jit_solution(47814192629271872)
XLA Ops:
  0.0 0.9 join.1
  0.9 1.7 %collective-permute-start.4 = (bf16[128,512]{1,0:T(8,128)(2,1)S(1)}, bf16[128,512]{1,0:T(8,128)(2,1)S(1)}, u32[]{:S(2)}, u32[]{:S(2)}) collective-permute-start(bf16[128,512]{1,0:T(8,128)(2,1)S(1)} %join.1), channel_id=1, source_target_pairs={{0,1},{1,0},{2,3},{3,2},{4,5},{5,4},{6,7},{7,6},{8,9},{9,8},{10,11... | collective-permute-start | bytes 393224 | tf_op jit(solution)/shard_map/ppermute | solution.py:402
  2.6 2.2 %collective-permute-start.5 = (bf16[128,512]{1,0:T(8,128)(2,1)S(1)}, bf16[128,512]{1,0:T(8,128)(2,1)S(1)}, u32[]{:S(2)}, u32[]{:S(2)}) collective-permute-start(bf16[128,512]{1,0:T(8,128)(2,1)S(1)} %join.1), channel_id=1, source_target_pairs={{0,3},{1,2},{2,1},{3,0},{4,7},{5,6},{6,5},{7,4},{8,11},{9,10},{10,... | collective-permute-start | bytes 393224 | tf_op jit(solution)/shard_map/ppermute | solution.py:402
  4.7 0.7 collective-permute-start.6
  6.1 0.0 copy-start.1
  6.1 0.7 copy-done.1
  6.8 3.9 %prepare.1 = bf16[144,512]{1,0:T(8,128)(2,1)S(1)} custom-call(s32[1]{0:T(128)S(6)} %copy.17.len_ref.refs_0_, s32[1,2,16]{2,1,0:T(2,128)S(1)} %copy-done.1, bf16[1,2,16,3584]{3,2,1,0:T(8,128)(2,1)} %refs_0_.2, bf16[3584,256]{1,0:T(8,128)(2,1)} %refs_1_.2, bf16[3584,256]{1,0:T(8,128)(2,1)} %refs_2_.1, bf16[128,256]{1,0:T(8,128)(2,1)} %refs_3_.1, ...), custom_call_target="tpu_custom_call" | custom-call | tf_op jit(solution)/shard_map/prepare/pallas_call | solution.py:457
  10.7 5.9 %collective-permute-start = (bf16[144,512]{1,0:T(8,128)(2,1)S(1)}, bf16[144,512]{1,0:T(8,128)(2,1)S(1)}, u32[]{:S(2)}, u32[]{:S(2)}) collective-permute-start(bf16[144,512]{1,0:T(8,128)(2,1)S(1)} %prepare.1), channel_id=1, source_target_pairs={{0,28},{1,29},{2,30},{3,31},{4,8},{5,9},{6,10},{7,11},{8,4},{9,5},... | collective-permute-start | bytes 442376 | tf_op jit(solution)/shard_map/ppermute | solution.py:402
  16.7 0.0 collective-permute-start.2
  16.7 0.0 copy-done
  16.7 0.6 queries.1.q_ref.refs_0_.refs_2_
  17.3 0.0 collective-permute-done.4
  17.3 0.0 collective-permute-done.5
  17.3 0.0 collective-permute-done.6
  17.4 2.1 %collective-permute-start.12 = (bf16[512,512]{1,0:T(8,128)(2,1)S(1)}, bf16[512,512]{1,0:T(8,128)(2,1)S(1)}, u32[]{:S(2)}, u32[]{:S(2)}) collective-permute-start(bf16[512,512]{1,0:T(8,128)(2,1)S(1)} %pad_maximum_fusion.piece), channel_id=1, source_target_pairs={{0,4},{1,5},{2,6},{3,7},{4,0},{5,1},{6,2},{7,3},{8,12},{9,13},{10,... | collective-permute-start | bytes 1572872 | tf_op jit(solution)/shard_map/ppermute | solution.py:402
  19.5 0.1 collective-permute-start.13
  19.6 1.9 %attend_first.1 = (f32[1568,256]{1,0:T(8,128)S(1)}, f32[1568,128]{1,0:T(8,128)S(1)}) custom-call(bf16[1568,128]{1,0:T(8,128)(2,1)S(1)} %queries.1.q_ref.refs_0_.refs_2_, bf16[512,512]{1,0:T(8,128)(2,1)S(1)} %pad_maximum_fusion.piece), custom_call_target="tpu_custom_call" | custom-call | flops 822083584 | bytes 524288 | tf_op jit(solution)/shard_map/attend_first/pallas_call | solution.py:278
  21.5 0.0 collective-permute-done
  21.5 1.1 %collective-permute-start.1 = (bf16[144,512]{1,0:T(8,128)(2,1)S(1)}, bf16[144,512]{1,0:T(8,128)(2,1)S(1)}, u32[]{:S(2)}, u32[]{:S(2)}) collective-permute-start(bf16[144,512]{1,0:T(8,128)(2,1)S(1)} %collective-permute-done), channel_id=1, source_target_pairs={{0,4},{1,5},{2,6},{3,7},{4,0},{5,1},{6,2},{7,3},{8,12},{9,13},{10,... | collective-permute-start | bytes 442376 | tf_op jit(solution)/shard_map/ppermute | solution.py:402
  22.6 0.9 collective-permute-done.2
  23.5 1.4 %collective-permute-start.3 = (bf16[144,512]{1,0:T(8,128)(2,1)S(1)}, bf16[144,512]{1,0:T(8,128)(2,1)S(1)}, u32[]{:S(2)}, u32[]{:S(2)}) collective-permute-start(bf16[144,512]{1,0:T(8,128)(2,1)S(1)} %collective-permute-done.2), channel_id=1, source_target_pairs={{0,28},{1,29},{2,30},{3,31},{4,8},{5,9},{6,10},{7,11},{8,4},{9,5},... | collective-permute-start | bytes 442376 | tf_op jit(solution)/shard_map/ppermute | solution.py:402
  24.9 10.9 %collective-permute-done.1 = bf16[144,512]{1,0:T(8,128)(2,1)S(1)} collective-permute-done((bf16[144,512]{1,0:T(8,128)(2,1)S(1)}, bf16[144,512]{1,0:T(8,128)(2,1)S(1)}, u32[]{:S(2)}, u32[]{:S(2)}) %collective-permute-start.1) | collective-permute-done | bytes 147488 | tf_op jit(solution)/shard_map/ppermute | solution.py:402
  35.8 0.3 collective-permute-done.3
  36.1 1.3 %collective-permute-start.8 = (bf16[144,512]{1,0:T(8,128)(2,1)S(1)}, bf16[144,512]{1,0:T(8,128)(2,1)S(1)}, u32[]{:S(2)}, u32[]{:S(2)}) collective-permute-start(bf16[144,512]{1,0:T(8,128)(2,1)S(1)} %collective-permute-done.1), channel_id=1, source_target_pairs={{0,28},{1,29},{2,30},{3,31},{4,8},{5,9},{6,10},{7,11},{8,4},{9,5},... | collective-permute-start | bytes 442376 | tf_op jit(solution)/shard_map/ppermute | solution.py:402
  37.5 0.1 collective-permute-start.7
  37.6 1.3 %collective-permute-start.16 = (bf16[720,512]{1,0:T(8,128)(2,1)S(1)}, bf16[720,512]{1,0:T(8,128)(2,1)S(1)}, u32[]{:S(2)}, u32[]{:S(2)}) collective-permute-start(bf16[720,512]{1,0:T(8,128)(2,1)S(1)} %constant_dynamic-update-slice_fusion.3), channel_id=1, source_target_pairs={{0,1},{1,0},{2,3},{3,2},{4,5},{5,4},{6,7},{7,6},{8,9},{9,8},{10,11... | collective-permute-start | bytes 2211848 | tf_op jit(solution)/shard_map/ppermute | solution.py:402
  38.9 3.6 %collective-permute-done.8 = bf16[144,512]{1,0:T(8,128)(2,1)S(1)} collective-permute-done((bf16[144,512]{1,0:T(8,128)(2,1)S(1)}, bf16[144,512]{1,0:T(8,128)(2,1)S(1)}, u32[]{:S(2)}, u32[]{:S(2)}) %collective-permute-start.8) | collective-permute-done | bytes 147488 | tf_op jit(solution)/shard_map/ppermute | solution.py:402
  42.5 2.4 %collective-permute-start.17 = (bf16[720,512]{1,0:T(8,128)(2,1)S(1)}, bf16[720,512]{1,0:T(8,128)(2,1)S(1)}, u32[]{:S(2)}, u32[]{:S(2)}) collective-permute-start(bf16[720,512]{1,0:T(8,128)(2,1)S(1)} %constant_dynamic-update-slice_fusion.3), channel_id=1, source_target_pairs={{0,3},{1,2},{2,1},{3,0},{4,7},{5,6},{6,5},{7,4},{8,11},{9,10},{10,... | collective-permute-start | bytes 2211848 | tf_op jit(solution)/shard_map/ppermute | solution.py:402
  44.8 0.0 collective-permute-done.7
  44.8 0.0 collective-permute-start.9
  44.8 0.0 collective-permute-done.12.refs_3_
  44.9 0.0 collective-permute-done.13.refs_4_
  44.9 2.1 %collective-permute-start.14 = (bf16[512,512]{1,0:T(8,128)(2,1)S(1)}, bf16[512,512]{1,0:T(8,128)(2,1)S(1)}, u32[]{:S(2)}, u32[]{:S(2)}) collective-permute-start(bf16[512,512]{1,0:T(8,128)(2,1)S(1)} %collective-permute-done.13.refs_4_), channel_id=1, source_target_pairs={{0,4},{1,5},{2,6},{3,7},{4,0},{5,1},{6,2},{7,3},{8,12},{9,13},{10,... | collective-permute-start | bytes 1572872 | tf_op jit(solution)/shard_map/ppermute | solution.py:402
  47.0 1.6 %collective-permute-start.15 = (bf16[512,512]{1,0:T(8,128)(2,1)S(1)}, bf16[512,512]{1,0:T(8,128)(2,1)S(1)}, u32[]{:S(2)}, u32[]{:S(2)}) collective-permute-start(bf16[512,512]{1,0:T(8,128)(2,1)S(1)} %collective-permute-done.12.refs_3_), channel_id=1, source_target_pairs={{0,28},{1,29},{2,30},{3,31},{4,8},{5,9},{6,10},{7,11},{8,4},{9,5},... | collective-permute-start | bytes 1572872 | tf_op jit(solution)/shard_map/ppermute | solution.py:402
  48.6 3.0 %collective-permute-done.9 = bf16[144,512]{1,0:T(8,128)(2,1)S(1)} collective-permute-done((bf16[144,512]{1,0:T(8,128)(2,1)S(1)}, bf16[144,512]{1,0:T(8,128)(2,1)S(1)}, u32[]{:S(2)}, u32[]{:S(2)}) %collective-permute-start.9) | collective-permute-done | bytes 147488 | tf_op jit(solution)/shard_map/ppermute | solution.py:402
  51.6 0.4 collective-permute-start.10
  52.0 12.5 %attend_ctx1.1 = (f32[1568,256]{1,0:T(8,128)S(1)}, f32[1568,128]{1,0:T(8,128)S(1)}) custom-call(bf16[1568,128]{1,0:T(8,128)(2,1)S(1)} %queries.1.q_ref.refs_0_.refs_2_, f32[1568,256]{1,0:T(8,128)S(1)} %get-tuple-element.55.refs_1_, f32[1568,128]{1,0:T(8,128)S(1)} %get-tuple-element.56.refs_2_, bf16[512,512]{1,0:T(8,128)(2,1)S(1)} %collective-permute-done.12.refs_3_, ...), custom_call_target="tpu_custom_call" | custom-call | flops 1644167168 | bytes 1048576 | tf_op jit(solution)/shard_map/attend_ctx1/pallas_call | solution.py:295
  64.5 0.0 collective-permute-done.16
  64.5 0.0 collective-permute-done.17
  64.5 0.0 collective-permute-done.14.refs_3_
  64.5 0.0 collective-permute-done.15.refs_4_
  64.5 0.1 collective-permute-start.18
  64.6 0.1 collective-permute-start.19
  64.7 0.1 collective-permute-start.11
  64.9 0.1 collective-permute-start.20
  65.0 0.3 collective-permute-done.10
  65.3 3.9 %collective-permute-start.21 = (bf16[288,512]{1,0:T(8,128)(2,1)S(1)}, bf16[288,512]{1,0:T(8,128)(2,1)S(1)}, u32[]{:S(2)}, u32[]{:S(2)}) collective-permute-start(bf16[288,512]{1,0:T(8,128)(2,1)S(1)} %slice.13), channel_id=1, source_target_pairs={{0,3},{1,2},{2,1},{3,0},{4,7},{5,6},{6,5},{7,4},{8,11},{9,10},{10,... | collective-permute-start | bytes 884744 | tf_op jit(solution)/shard_map/ppermute | solution.py:402
  69.2 4.4 %attend_span1.1 = (f32[1568,256]{1,0:T(8,128)S(1)}, f32[1568,128]{1,0:T(8,128)S(1)}, bf16[15,16,512]{2,1,0:T(8,128)(2,1)S(1)}, bf16[15,16,512]{2,1,0:T(8,128)(2,1)S(1)}) custom-call(bf16[1568,128]{1,0:T(8,128)(2,1)S(1)} %queries.1.q_ref.refs_0_.refs_2_, f32[1568,256]{1,0:T(8,128)S(1)} %get-tuple-element.63.refs_1_, ...), custom_call_target="tpu_custom_call" | custom-call | flops 2697461760 | bytes 1720320 | tf_op jit(solution)/shard_map/attend_span1/pallas_call | solution.py:295
  73.6 2.7 %attend_ctx2.1 = (f32[1568,256]{1,0:T(8,128)S(1)}, f32[1568,128]{1,0:T(8,128)S(1)}) custom-call(bf16[1568,128]{1,0:T(8,128)(2,1)S(1)} %queries.1.q_ref.refs_0_.refs_2_, f32[1568,256]{1,0:T(8,128)S(1)} %get-tuple-element.67.refs_1_, f32[1568,128]{1,0:T(8,128)S(1)} %get-tuple-element.68.refs_2_, bf16[512,512]{1,0:T(8,128)(2,1)S(1)} %collective-permute-done.14.refs_3_, ...), custom_call_target="tpu_custom_call" | custom-call | flops 1644167168 | bytes 1048576 | tf_op jit(solution)/shard_map/attend_ctx2/pallas_call | solution.py:295
  76.3 0.0 collective-permute-done.11
  76.3 0.0 collective-permute-done.18.refs_3_
  76.3 0.0 collective-permute-done.19.refs_4_
  76.3 2.1 %collective-permute-start.24 = (bf16[512,512]{1,0:T(8,128)(2,1)S(1)}, bf16[512,512]{1,0:T(8,128)(2,1)S(1)}, u32[]{:S(2)}, u32[]{:S(2)}) collective-permute-start(bf16[512,512]{1,0:T(8,128)(2,1)S(1)} %collective-permute-done.19.refs_4_), channel_id=1, source_target_pairs={{0,4},{1,5},{2,6},{3,7},{4,0},{5,1},{6,2},{7,3},{8,12},{9,13},{10,... | collective-permute-start | bytes 1572872 | tf_op jit(solution)/shard_map/ppermute | solution.py:402
  78.4 0.7 collective-permute-start.23
  79.1 0.3 collective-permute-start.22
  79.5 0.1 collective-permute-done.21
  79.6 0.0 collective-permute-done.20
  79.6 2.7 %attend_span2.1 = (f32[1568,256]{1,0:T(8,128)S(1)}, f32[1568,128]{1,0:T(8,128)S(1)}, bf16[8,16,512]{2,1,0:T(8,128)(2,1)S(1)}, bf16[8,16,512]{2,1,0:T(8,128)(2,1)S(1)}) custom-call(bf16[1568,128]{1,0:T(8,128)(2,1)S(1)} %queries.1.q_ref.refs_0_.refs_2_, f32[1568,256]{1,0:T(8,128)S(1)} %get-tuple-element.71.refs_1_, f32[1568,128]{1,0:T(8,128)S(1)} %get-tuple-element.72.refs_2_, ...), custom_call_target="tpu_custom_call" | custom-call | flops 1438646272 | bytes 917504 | tf_op jit(solution)/shard_map/attend_span2/pallas_call | solution.py:295
  82.3 2.7 %attend_ctx3.1 = (f32[1568,256]{1,0:T(8,128)S(1)}, f32[1568,128]{1,0:T(8,128)S(1)}) custom-call(bf16[1568,128]{1,0:T(8,128)(2,1)S(1)} %queries.1.q_ref.refs_0_.refs_2_, f32[1568,256]{1,0:T(8,128)S(1)} %get-tuple-element.73.refs_1_, f32[1568,128]{1,0:T(8,128)S(1)} %get-tuple-element.74.refs_2_, bf16[512,512]{1,0:T(8,128)(2,1)S(1)} %collective-permute-done.18.refs_3_, ...), custom_call_target="tpu_custom_call" | custom-call | flops 1644167168 | bytes 1048576 | tf_op jit(solution)/shard_map/attend_ctx3/pallas_call | solution.py:295
  85.0 0.0 collective-permute-done.22
  85.1 1.4 %collective-permute-done.23 = bf16[288,512]{1,0:T(8,128)(2,1)S(1)} collective-permute-done((bf16[288,512]{1,0:T(8,128)(2,1)S(1)}, bf16[288,512]{1,0:T(8,128)(2,1)S(1)}, u32[]{:S(2)}, u32[]{:S(2)}) %collective-permute-start.23) | collective-permute-done | bytes 294944 | tf_op jit(solution)/shard_map/ppermute | solution.py:402
  86.5 2.7 %attend_span3.1 = (f32[1568,256]{1,0:T(8,128)S(1)}, f32[1568,128]{1,0:T(8,128)S(1)}, bf16[9,16,512]{2,1,0:T(8,128)(2,1)S(1)}, bf16[9,16,512]{2,1,0:T(8,128)(2,1)S(1)}) custom-call(bf16[1568,128]{1,0:T(8,128)(2,1)S(1)} %queries.1.q_ref.refs_0_.refs_2_, f32[1568,256]{1,0:T(8,128)S(1)} %get-tuple-element.77.refs_1_, f32[1568,128]{1,0:T(8,128)S(1)} %get-tuple-element.78.refs_2_, ...), custom_call_target="tpu_custom_call" | custom-call | flops 1618477056 | bytes 1032192 | tf_op jit(solution)/shard_map/attend_span3/pallas_call | solution.py:295
  89.2 0.0 collective-permute-done.24.refs_5_
  89.2 5.6 %attend_last.1 = bf16[2,128,1792]{2,1,0:T(8,128)(2,1)} custom-call(s32[1]{0:T(128)S(6)} %copy.17.len_ref.refs_0_, s32[1,2,16]{2,1,0:T(2,128)S(1)} %copy-done.2, bf16[1568,128]{1,0:T(8,128)(2,1)S(1)} %queries.1.q_ref.refs_0_.refs_2_, f32[1568,256]{1,0:T(8,128)S(1)} %get-tuple-element.81.refs_3_, f32[1568,128]{1,0:T(8,128)S(1)} %get-tuple-element.82.refs_4_, ...), custom_call_target="tpu_custom_call" | custom-call | flops 2466250752 | bytes 1572864 | tf_op jit(solution)/shard_map/attend_last/pallas_call | solution.py:372
  (16 shorter events, 0.2 us)
Async XLA Ops:
  0.9 16.4 %collective-permute-start.4 = (bf16[128,512]{1,0:T(8,128)(2,1)S(1)}, bf16[128,512]{1,0:T(8,128)(2,1)S(1)}, u32[]{:S(2)}, u32[]{:S(2)}) collective-permute-start(bf16[128,512]{1,0:T(8,128)(2,1)S(1)} %join.1), channel_id=1, source_target_pairs={{0,1},{1,0},{2,3},{3,2},{4,5},{5,4},{6,7},{7,6},{8,9},{9,8},{10,11... | collective-permute-start | bytes 393224 | tf_op jit(solution)/shard_map/ppermute | solution.py:402
  2.6 14.7 %collective-permute-start.5 = (bf16[128,512]{1,0:T(8,128)(2,1)S(1)}, bf16[128,512]{1,0:T(8,128)(2,1)S(1)}, u32[]{:S(2)}, u32[]{:S(2)}) collective-permute-start(bf16[128,512]{1,0:T(8,128)(2,1)S(1)} %join.1), channel_id=1, source_target_pairs={{0,3},{1,2},{2,1},{3,0},{4,7},{5,6},{6,5},{7,4},{8,11},{9,10},{10,... | collective-permute-start | bytes 393224 | tf_op jit(solution)/shard_map/ppermute | solution.py:402
  4.7 12.6 %collective-permute-start.6 = (bf16[128,512]{1,0:T(8,128)(2,1)S(1)}, bf16[128,512]{1,0:T(8,128)(2,1)S(1)}, u32[]{:S(2)}, u32[]{:S(2)}) collective-permute-start(bf16[128,512]{1,0:T(8,128)(2,1)S(1)} %join.1), channel_id=1, source_target_pairs={{0,2},{1,3},{2,0},{3,1},{4,6},{5,7},{6,4},{7,5},{8,10},{9,11},{10,... | collective-permute-start | bytes 393224 | tf_op jit(solution)/shard_map/ppermute | solution.py:402
  6.1 0.7 copy-start.1
  6.8 9.9 %copy-start = (bf16[128,1792]{1,0:T(8,128)(2,1)S(1)}, bf16[128,1792]{1,0:T(8,128)(2,1)}, u32[]{:S(2)}) copy-start(bf16[128,1792]{1,0:T(8,128)(2,1)} %mq_ref.1) | copy-start | bytes 1376260
  10.7 10.8 %collective-permute-start = (bf16[144,512]{1,0:T(8,128)(2,1)S(1)}, bf16[144,512]{1,0:T(8,128)(2,1)S(1)}, u32[]{:S(2)}, u32[]{:S(2)}) collective-permute-start(bf16[144,512]{1,0:T(8,128)(2,1)S(1)} %prepare.1), channel_id=1, source_target_pairs={{0,28},{1,29},{2,30},{3,31},{4,8},{5,9},{6,10},{7,11},{8,4},{9,5},... | collective-permute-start | bytes 442376 | tf_op jit(solution)/shard_map/ppermute | solution.py:402
  16.7 6.8 %collective-permute-start.2 = (bf16[144,512]{1,0:T(8,128)(2,1)S(1)}, bf16[144,512]{1,0:T(8,128)(2,1)S(1)}, u32[]{:S(2)}, u32[]{:S(2)}) collective-permute-start(bf16[144,512]{1,0:T(8,128)(2,1)S(1)} %prepare.1), channel_id=1, source_target_pairs={{0,4},{1,5},{2,6},{3,7},{4,0},{5,1},{6,2},{7,3},{8,12},{9,13},{10,... | collective-permute-start | bytes 442376 | tf_op jit(solution)/shard_map/ppermute | solution.py:402
  17.4 27.5 %collective-permute-start.12 = (bf16[512,512]{1,0:T(8,128)(2,1)S(1)}, bf16[512,512]{1,0:T(8,128)(2,1)S(1)}, u32[]{:S(2)}, u32[]{:S(2)}) collective-permute-start(bf16[512,512]{1,0:T(8,128)(2,1)S(1)} %pad_maximum_fusion.piece), channel_id=1, source_target_pairs={{0,4},{1,5},{2,6},{3,7},{4,0},{5,1},{6,2},{7,3},{8,12},{9,13},{10,... | collective-permute-start | bytes 1572872 | tf_op jit(solution)/shard_map/ppermute | solution.py:402
  19.5 25.4 %collective-permute-start.13 = (bf16[512,512]{1,0:T(8,128)(2,1)S(1)}, bf16[512,512]{1,0:T(8,128)(2,1)S(1)}, u32[]{:S(2)}, u32[]{:S(2)}) collective-permute-start(bf16[512,512]{1,0:T(8,128)(2,1)S(1)} %pad_maximum_fusion.piece), channel_id=1, source_target_pairs={{0,28},{1,29},{2,30},{3,31},{4,8},{5,9},{6,10},{7,11},{8,4},{9,5},... | collective-permute-start | bytes 1572872 | tf_op jit(solution)/shard_map/ppermute | solution.py:402
  21.5 14.3 %collective-permute-start.1 = (bf16[144,512]{1,0:T(8,128)(2,1)S(1)}, bf16[144,512]{1,0:T(8,128)(2,1)S(1)}, u32[]{:S(2)}, u32[]{:S(2)}) collective-permute-start(bf16[144,512]{1,0:T(8,128)(2,1)S(1)} %collective-permute-done), channel_id=1, source_target_pairs={{0,4},{1,5},{2,6},{3,7},{4,0},{5,1},{6,2},{7,3},{8,12},{9,13},{10,... | collective-permute-start | bytes 442376 | tf_op jit(solution)/shard_map/ppermute | solution.py:402
  23.5 12.6 %collective-permute-start.3 = (bf16[144,512]{1,0:T(8,128)(2,1)S(1)}, bf16[144,512]{1,0:T(8,128)(2,1)S(1)}, u32[]{:S(2)}, u32[]{:S(2)}) collective-permute-start(bf16[144,512]{1,0:T(8,128)(2,1)S(1)} %collective-permute-done.2), channel_id=1, source_target_pairs={{0,28},{1,29},{2,30},{3,31},{4,8},{5,9},{6,10},{7,11},{8,4},{9,5},... | collective-permute-start | bytes 442376 | tf_op jit(solution)/shard_map/ppermute | solution.py:402
  36.1 6.4 %collective-permute-start.8 = (bf16[144,512]{1,0:T(8,128)(2,1)S(1)}, bf16[144,512]{1,0:T(8,128)(2,1)S(1)}, u32[]{:S(2)}, u32[]{:S(2)}) collective-permute-start(bf16[144,512]{1,0:T(8,128)(2,1)S(1)} %collective-permute-done.1), channel_id=1, source_target_pairs={{0,28},{1,29},{2,30},{3,31},{4,8},{5,9},{6,10},{7,11},{8,4},{9,5},... | collective-permute-start | bytes 442376 | tf_op jit(solution)/shard_map/ppermute | solution.py:402
  37.5 7.4 %collective-permute-start.7 = (bf16[144,512]{1,0:T(8,128)(2,1)S(1)}, bf16[144,512]{1,0:T(8,128)(2,1)S(1)}, u32[]{:S(2)}, u32[]{:S(2)}) collective-permute-start(bf16[144,512]{1,0:T(8,128)(2,1)S(1)} %collective-permute-done.3), channel_id=1, source_target_pairs={{0,4},{1,5},{2,6},{3,7},{4,0},{5,1},{6,2},{7,3},{8,12},{9,13},{10,... | collective-permute-start | bytes 442376 | tf_op jit(solution)/shard_map/ppermute | solution.py:402
  37.6 26.9 %collective-permute-start.16 = (bf16[720,512]{1,0:T(8,128)(2,1)S(1)}, bf16[720,512]{1,0:T(8,128)(2,1)S(1)}, u32[]{:S(2)}, u32[]{:S(2)}) collective-permute-start(bf16[720,512]{1,0:T(8,128)(2,1)S(1)} %constant_dynamic-update-slice_fusion.3), channel_id=1, source_target_pairs={{0,1},{1,0},{2,3},{3,2},{4,5},{5,4},{6,7},{7,6},{8,9},{9,8},{10,11... | collective-permute-start | bytes 2211848 | tf_op jit(solution)/shard_map/ppermute | solution.py:402
  42.5 22.0 %collective-permute-start.17 = (bf16[720,512]{1,0:T(8,128)(2,1)S(1)}, bf16[720,512]{1,0:T(8,128)(2,1)S(1)}, u32[]{:S(2)}, u32[]{:S(2)}) collective-permute-start(bf16[720,512]{1,0:T(8,128)(2,1)S(1)} %constant_dynamic-update-slice_fusion.3), channel_id=1, source_target_pairs={{0,3},{1,2},{2,1},{3,0},{4,7},{5,6},{6,5},{7,4},{8,11},{9,10},{10,... | collective-permute-start | bytes 2211848 | tf_op jit(solution)/shard_map/ppermute | solution.py:402
  44.8 6.8 %collective-permute-start.9 = (bf16[144,512]{1,0:T(8,128)(2,1)S(1)}, bf16[144,512]{1,0:T(8,128)(2,1)S(1)}, u32[]{:S(2)}, u32[]{:S(2)}) collective-permute-start(bf16[144,512]{1,0:T(8,128)(2,1)S(1)} %collective-permute-done.8), channel_id=1, source_target_pairs={{0,4},{1,5},{2,6},{3,7},{4,0},{5,1},{6,2},{7,3},{8,12},{9,13},{10,... | collective-permute-start | bytes 442376 | tf_op jit(solution)/shard_map/ppermute | solution.py:402
  44.9 19.6 %collective-permute-start.14 = (bf16[512,512]{1,0:T(8,128)(2,1)S(1)}, bf16[512,512]{1,0:T(8,128)(2,1)S(1)}, u32[]{:S(2)}, u32[]{:S(2)}) collective-permute-start(bf16[512,512]{1,0:T(8,128)(2,1)S(1)} %collective-permute-done.13.refs_4_), channel_id=1, source_target_pairs={{0,4},{1,5},{2,6},{3,7},{4,0},{5,1},{6,2},{7,3},{8,12},{9,13},{10,... | collective-permute-start | bytes 1572872 | tf_op jit(solution)/shard_map/ppermute | solution.py:402
  47.0 17.5 %collective-permute-start.15 = (bf16[512,512]{1,0:T(8,128)(2,1)S(1)}, bf16[512,512]{1,0:T(8,128)(2,1)S(1)}, u32[]{:S(2)}, u32[]{:S(2)}) collective-permute-start(bf16[512,512]{1,0:T(8,128)(2,1)S(1)} %collective-permute-done.12.refs_3_), channel_id=1, source_target_pairs={{0,28},{1,29},{2,30},{3,31},{4,8},{5,9},{6,10},{7,11},{8,4},{9,5},... | collective-permute-start | bytes 1572872 | tf_op jit(solution)/shard_map/ppermute | solution.py:402
  51.6 13.6 %collective-permute-start.10 = (bf16[432,512]{1,0:T(8,128)(2,1)S(1)}, bf16[432,512]{1,0:T(8,128)(2,1)S(1)}, u32[]{:S(2)}, u32[]{:S(2)}) collective-permute-start(bf16[432,512]{1,0:T(8,128)(2,1)S(1)} %constant_dynamic-update-slice_fusion), channel_id=1, source_target_pairs={{0,1},{1,0},{2,3},{3,2},{4,5},{5,4},{6,7},{7,6},{8,9},{9,8},{10,11... | collective-permute-start | bytes 1327112 | tf_op jit(solution)/shard_map/ppermute | solution.py:402
  64.5 11.8 %collective-permute-start.18 = (bf16[512,512]{1,0:T(8,128)(2,1)S(1)}, bf16[512,512]{1,0:T(8,128)(2,1)S(1)}, u32[]{:S(2)}, u32[]{:S(2)}) collective-permute-start(bf16[512,512]{1,0:T(8,128)(2,1)S(1)} %collective-permute-done.15.refs_4_), channel_id=1, source_target_pairs={{0,4},{1,5},{2,6},{3,7},{4,0},{5,1},{6,2},{7,3},{8,12},{9,13},{10,... | collective-permute-start | bytes 1572872 | tf_op jit(solution)/shard_map/ppermute | solution.py:402
  64.6 11.7 %collective-permute-start.19 = (bf16[512,512]{1,0:T(8,128)(2,1)S(1)}, bf16[512,512]{1,0:T(8,128)(2,1)S(1)}, u32[]{:S(2)}, u32[]{:S(2)}) collective-permute-start(bf16[512,512]{1,0:T(8,128)(2,1)S(1)} %collective-permute-done.14.refs_3_), channel_id=1, source_target_pairs={{0,28},{1,29},{2,30},{3,31},{4,8},{5,9},{6,10},{7,11},{8,4},{9,5},... | collective-permute-start | bytes 1572872 | tf_op jit(solution)/shard_map/ppermute | solution.py:402
  64.7 11.6 %collective-permute-start.11 = (bf16[432,512]{1,0:T(8,128)(2,1)S(1)}, bf16[432,512]{1,0:T(8,128)(2,1)S(1)}, u32[]{:S(2)}, u32[]{:S(2)}) collective-permute-start(bf16[432,512]{1,0:T(8,128)(2,1)S(1)} %constant_dynamic-update-slice_fusion), channel_id=1, source_target_pairs={{0,3},{1,2},{2,1},{3,0},{4,7},{5,6},{6,5},{7,4},{8,11},{9,10},{10,... | collective-permute-start | bytes 1327112 | tf_op jit(solution)/shard_map/ppermute | solution.py:402
  64.9 14.7 %collective-permute-start.20 = (bf16[432,512]{1,0:T(8,128)(2,1)S(1)}, bf16[432,512]{1,0:T(8,128)(2,1)S(1)}, u32[]{:S(2)}, u32[]{:S(2)}) collective-permute-start(bf16[432,512]{1,0:T(8,128)(2,1)S(1)} %slice.12), channel_id=1, source_target_pairs={{0,1},{1,0},{2,3},{3,2},{4,5},{5,4},{6,7},{7,6},{8,9},{9,8},{10,11... | collective-permute-start | bytes 1327112 | tf_op jit(solution)/shard_map/ppermute | solution.py:402
  65.3 14.3 %collective-permute-start.21 = (bf16[288,512]{1,0:T(8,128)(2,1)S(1)}, bf16[288,512]{1,0:T(8,128)(2,1)S(1)}, u32[]{:S(2)}, u32[]{:S(2)}) collective-permute-start(bf16[288,512]{1,0:T(8,128)(2,1)S(1)} %slice.13), channel_id=1, source_target_pairs={{0,3},{1,2},{2,1},{3,0},{4,7},{5,6},{6,5},{7,4},{8,11},{9,10},{10,... | collective-permute-start | bytes 884744 | tf_op jit(solution)/shard_map/ppermute | solution.py:402
  76.3 12.9 %collective-permute-start.24 = (bf16[512,512]{1,0:T(8,128)(2,1)S(1)}, bf16[512,512]{1,0:T(8,128)(2,1)S(1)}, u32[]{:S(2)}, u32[]{:S(2)}) collective-permute-start(bf16[512,512]{1,0:T(8,128)(2,1)S(1)} %collective-permute-done.19.refs_4_), channel_id=1, source_target_pairs={{0,4},{1,5},{2,6},{3,7},{4,0},{5,1},{6,2},{7,3},{8,12},{9,13},{10,... | collective-permute-start | bytes 1572872 | tf_op jit(solution)/shard_map/ppermute | solution.py:402
  78.4 8.0 %collective-permute-start.23 = (bf16[288,512]{1,0:T(8,128)(2,1)S(1)}, bf16[288,512]{1,0:T(8,128)(2,1)S(1)}, u32[]{:S(2)}, u32[]{:S(2)}) collective-permute-start(bf16[288,512]{1,0:T(8,128)(2,1)S(1)} %slice.15), channel_id=1, source_target_pairs={{0,3},{1,2},{2,1},{3,0},{4,7},{5,6},{6,5},{7,4},{8,11},{9,10},{10,... | collective-permute-start | bytes 884744 | tf_op jit(solution)/shard_map/ppermute | solution.py:402
  79.1 5.9 %collective-permute-start.22 = (bf16[144,512]{1,0:T(8,128)(2,1)S(1)}, bf16[144,512]{1,0:T(8,128)(2,1)S(1)}, u32[]{:S(2)}, u32[]{:S(2)}) collective-permute-start(bf16[144,512]{1,0:T(8,128)(2,1)S(1)} %slice.14), channel_id=1, source_target_pairs={{0,1},{1,0},{2,3},{3,2},{4,5},{5,4},{6,7},{7,6},{8,9},{9,8},{10,11... | collective-permute-start | bytes 442376 | tf_op jit(solution)/shard_map/ppermute | solution.py:402
  86.5 2.7 %copy-start.2 = (s32[1,2,16]{2,1,0:T(2,128)S(1)}, s32[1,2,16]{2,1,0:T(2,128)}, u32[]{:S(2)}) copy-start(s32[1,2,16]{2,1,0:T(2,128)} %refs_1_.3) | copy-start | bytes 388
where the time goes:
time: 95 us; the launch traced here: 94.8 us
  Pallas kernels  40.6 us (43%)
  starting transfers between devices  31.7 us (33%)
  waiting for transfers between devices  20.6 us (22%)
  between operations  1 us (1%)
    ppermute x25, starting transfers between devices, exchange(): return lax.ppermute(x, 'blk', pairs)  31.7 us
    pallas_call x6, Pallas kernels, attend_piece(): pl.pallas_call(functools.partial(piece_kernel, span, len(pieces)), out_sh...  27.7 us
    ppermute x25, waiting for transfers between devices, exchange(): return lax.ppermute(x, 'blk', pairs)  20.6 us
    pallas_call x1, Pallas kernels, attend_last(): pl.pallas_call(functools.partial(last_kernel, len(pieces), len(olds)), ou...  5.59 us
    pallas_call x1, Pallas kernels, per_device(): pl.pallas_call(prepare_kernel, out_shape=jax.ShapeDtypeStruct((SLOTS + CO...  3.94 us
    pallas_call x1, Pallas kernels, attend_first(): pl.pallas_call(first_kernel, out_shape=STATE, in_specs=[VMEM] * 2, out_sp...  1.92 us
  transfers between devices with their start and end apart: 25, of which 8 were waited for; matrix products, arithmetic and copies ran while one was open for 0% of the time, Pallas kernels for 36%

commit v1 on v0

--- a/solution.py
+++ b/solution.py
@@ -138,7 +138,7 @@
     return jnp.where(marked, zero, values), jnp.where(marked, zero, jnp.ones_like(values))
 
 
-def gather_rows(refs, block, keys, values):
+def gather_rows(refs, start, block, keys, values):
     at = 0
     for ref in refs:
         flat = len(ref.shape) == 2
@@ -148,7 +148,7 @@
             if flat:
                 got = ref[:, cols]
             else:
-                got = ref[:, :block, cols].reshape(count, HEAD)
+                got = ref[:, start : start + block, cols].reshape(count, HEAD)
             rows = slice(at, at + count)
             if index < GROUPS:
                 keys[rows, cols] = got
@@ -192,8 +192,9 @@
     return jnp.max(jnp.where(total < LIMIT, 0.0, 1.0)) > 0.5
 
 
-def first_kernel(q_ref, piece, acc, top, keys, values):
-    gather_rows([piece], COMMON, keys, values)
+def first_kernel(q_ref, *refs):
+    *pieces, acc, top, keys, values = refs
+    gather_rows(pieces, 0, COMMON, keys, values)
 
     def one_group(group, _):
         for head in range(PER_GROUP):
@@ -217,9 +218,11 @@
     acc, top = refs.pop(0), refs.pop(0)
     old, new = (refs.pop(0), refs.pop(0)) if span else (None, None)
     keys, values = refs
-    gather_rows(pieces, COMMON, keys, values)
+    gather_rows(pieces, 0, COMMON, keys, values)
     at = 0
-    for piece in pieces if span else ():
+    for piece in pieces:
+        if len(piece.shape) == 2:
+            continue
         blocks = piece.shape[0]
         old[at : at + blocks] = piece[:, COMMON:SLOTS, :]
         new[at : at + blocks] = piece[:, SLOTS:, :]
@@ -257,7 +260,7 @@
 def estimate(keys):
     work = HEADS * COMMON * keys
     return pl.CostEstimate(
-        flops=8 * work * HEAD, bytes_accessed=keys * PAIR * 2, transcendentals=work
+        flops=14 * work * HEAD, bytes_accessed=keys * PAIR * 2, transcendentals=work
     )
 
 
@@ -274,26 +277,28 @@
     ]
 
 
-def attend_first(queries, piece):
+def attend_first(queries, pieces):
+    rows = sum(piece.shape[0] for piece in pieces)
     return pl.pallas_call(
         first_kernel,
         out_shape=STATE,
-        in_specs=[VMEM] * 2,
+        in_specs=[VMEM] * (1 + len(pieces)),
         out_specs=[VMEM] * 2,
-        scratch_shapes=padded(piece.shape[0]),
+        scratch_shapes=padded(rows),
         compiler_params=vmem_params(24),
-        cost_estimate=estimate(piece.shape[0]),
+        cost_estimate=estimate(rows),
         name="attend_first",
-    )(queries, piece)
-
-
-def attend_piece(name, queries, state, pieces, span=False):
-    rows = sum(piece.shape[0] for piece in pieces) * (COMMON if span else 1)
+    )(queries, *pieces)
+
+
+def attend_piece(name, queries, state, pieces):
+    blocks = sum(piece.shape[0] for piece in pieces if len(piece.shape) == 3)
+    rows = blocks * COMMON + sum(piece.shape[0] for piece in pieces if len(piece.shape) == 2)
     outs = list(STATE)
-    if span:
-        outs += [jax.ShapeDtypeStruct((rows // COMMON, COMMIT, PAIR), BF16)] * 2
+    if blocks:
+        outs += [jax.ShapeDtypeStruct((blocks, COMMIT, PAIR), BF16)] * 2
     got = pl.pallas_call(
-        functools.partial(piece_kernel, span, len(pieces)),
+        functools.partial(piece_kernel, blocks > 0, len(pieces)),
         out_shape=outs,
         in_specs=[VMEM] * (3 + len(pieces)),
         out_specs=[VMEM] * len(outs),
@@ -315,8 +320,14 @@
     sources = [[refs.pop(0) for _ in range(n)] for n in (count, extra_count, extra_count)]
     out_ref, rows_out, done, largest = [refs.pop(0) for _ in range(4)]
     held = [(refs.pop(0), refs.pop(0)) for _ in range(3)]
-    for source, (keys, values) in zip(sources, held):
-        gather_rows(source, COMMIT, keys, values)
+    ends = sources[0]
+    spans = ((0, COMMON), (COMMON, COMMIT), (SLOTS, COMMIT))
+    for source, (start, size), (keys, values) in zip(sources, spans, held):
+        at = 0
+        if start:
+            at = sum(ref.shape[0] for ref in source) * COMMIT
+            gather_rows(source, 0, COMMIT, keys.at[:at], values.at[:at])
+        gather_rows(ends, start, size, keys.at[at:], values.at[at:])
     rows_out[:, COMMON:, :] = jnp.zeros((2, COMMIT, HEADS * HEAD), BF16)
 
     def one_group(group, _):
@@ -367,8 +378,9 @@
 
 
 def attend_last(span_len, commit_pos, queries, state, pieces, olds, news):
-    extra = sum(part.shape[0] for part in olds) * COMMIT
-    sizes = [sum(piece.shape[0] for piece in pieces), extra, extra]
+    blocks = sum(piece.shape[0] for piece in pieces)
+    extra = (blocks + sum(part.shape[0] for part in olds)) * COMMIT
+    sizes = [blocks * COMMON, extra, extra]
     return pl.pallas_call(
         functools.partial(last_kernel, len(pieces), len(olds)),
         out_shape=jax.ShapeDtypeStruct((2, SLOTS, HEADS * HEAD), BF16),
@@ -452,7 +464,7 @@
         compiler_params=vmem_params(4),
         name="join",
     )(in_hbm(ctx_keys), in_hbm(ctx_values))
-    near = [y_even(ctx), y_odd(ctx), y_far(ctx)]
+    ring1 = round_z(ctx, ctx)
     held = [in_hbm(x) for x in (commit_emb, w_key, w_value, span_keys, span_values)]
     span = pl.pallas_call(
         prepare_kernel,
@@ -462,6 +474,7 @@
         scratch_shapes=[pltpu.VMEM(x.shape, x.dtype) for x in held]
         + [pltpu.SemaphoreType.DMA((len(held),))],
         compiler_params=vmem_params(12),
+        cost_estimate=pl.CostEstimate(flops=1 << 28, bytes_accessed=12 << 20, transcendentals=0),
         name="prepare",
     )(span_len, commit_pos, *held)
     queries = pl.pallas_call(
@@ -473,47 +486,41 @@
         name="queries",
     )(commit_pos, middle_queries)
 
-    near1 = round_z(span, span)
-    near2 = round_z(*near1)
-
     def blocks(x):
         return x.reshape(-1, SLOTS + COMMIT, PAIR)
 
-    ctx4 = jnp.concatenate([ctx] + near)
-    state = attend_first(queries, ctx4)
-    *near2, state = together((*near2, state))
-    near3 = round_z(*near2)
-    far = z_even(near3[1])
-    first = jnp.concatenate([span, *near1, *near2])
-    second = jnp.concatenate([*near3, far])
-    first_y = y_even(first), y_odd(first)
-    ctx1 = round_z(ctx4, ctx4)
-    *ctx1, state = together((*ctx1, state))
-    ctx2 = round_z(*ctx1)
-    state, _ = attend_piece("attend_ctx1", queries, state, ctx1)
-    *first_y, state = together((*first_y, state))
-    cut = 3 * (SLOTS + COMMIT)
-    first_far = y_even(first_y[1][:cut]), y_odd(first_y[0][cut:])
-    *ctx2, state = together((*ctx2, state))
-    ctx3 = round_z(*ctx2)
-    second_y = y_even(second), y_odd(second)
-    state, extra1 = attend_piece(
-        "attend_span1", queries, state, [blocks(x) for x in (first, *first_y)], True
+    ring1, span = together((ring1, span))
+    ring2 = round_z(*ring1)
+    near = [y_even(span), y_odd(span), y_far(span)]
+    ring3 = round_z(*ring2)
+    span4 = jnp.concatenate([span] + near)
+    span1 = round_z(span4, span4)
+    state = attend_first(queries, [*ring1, *ring2])
+    ring4 = z_even(ring3[1])
+    column = jnp.concatenate([ctx, *ring1, *ring2, *ring3, ring4])
+    beside = y_even(column), y_odd(column)
+    span1, state = together((span1, state))
+    span2 = round_z(*span1)
+    state, extra0 = attend_piece(
+        "attend_mixed", queries, state, [ctx, *ring3, ring4, blocks(span4)]
     )
-    state, _ = attend_piece("attend_ctx2", queries, state, ctx2)
-    second_y, ctx3, state = together((second_y, ctx3, state))
-    cut = SLOTS + COMMIT
-    second_far = y_even(second_y[1][:cut]), y_odd(second_y[0][cut:])
-    ends = [z_even(ctx3[1])]
-    state, extra2 = attend_piece(
-        "attend_span2", queries, state, [blocks(x) for x in (*first_far, second)], True
-    )
-    state, _ = attend_piece("attend_ctx3", queries, state, ctx3)
-    state, extra3 = attend_piece(
-        "attend_span3", queries, state, [blocks(x) for x in (*second_y, *second_far)], True
-    )
-    olds = [extra[0] for extra in (extra1, extra2, extra3)]
-    news = [extra[1] for extra in (extra1, extra2, extra3)]
+    span2, state = together((span2, state))
+    span3 = round_z(*span2)
+    state, extra1 = attend_piece("attend_span1", queries, state, [blocks(x) for x in span1])
+    beside, state = together((beside, state))
+    half = column.shape[0] // 2
+    across = y_even(beside[1][:half]), y_odd(beside[0][half:])
+    state, _ = attend_piece("attend_ctx1", queries, state, [beside[0]])
+    state, _ = attend_piece("attend_ctx2", queries, state, [beside[1]])
+    state, extra2 = attend_piece("attend_span2", queries, state, [blocks(x) for x in span2])
+    span3, state = together((span3, state))
+    half = span4.shape[0] // 2
+    ends = z_even(span3[1][:half]), z_odd(span3[0][half:])
+    state, _ = attend_piece("attend_ctx3", queries, state, across)
+    state, extra3 = attend_piece("attend_span3", queries, state, [blocks(x) for x in span3])
+    olds = [extra[0] for extra in (extra0, extra1, extra2, extra3)]
+    news = [extra[1] for extra in (extra0, extra1, extra2, extra3)]
+    ends = [blocks(x) for x in ends]
     return attend_last(span_len, commit_pos, queries, state, ends, olds, news)
 
 

time: 95 us -> 104 us (1.095)
  waiting for transfers between devices: 20.6 us -> 29.8 us
  starting transfers between devices: 31.7 us -> 30.4 us
    ppermute x25 -> x22, waiting for transfers between devices: 20.6 us -> 29.8 us  [exchange(): return lax.ppermute(x, 'blk', pairs)]
    ppermute x25 -> x22, starting transfers between devices: 31.7 us -> 30.4 us  [exchange(): return lax.ppermute(x, 'blk', pairs)]
    pallas_call x7 -> x8, Pallas kernels: 29.6 us -> 30.7 us  [the longest x7 28.8 us: attend_piece(): pl.pallas_call(functools.partial(piece_kernel, blocks > 0, len(pieces)),...]
  transfers between devices with their start and end apart: 25 -> 22, of which waited for: 8 -> 9; matrix products, arithmetic and copies ran while one was open for 0% -> 0% of each run, Pallas kernels for 36% -> 34%
where the time goes in v1:
time: 104 us
  Pallas kernels  41.6 us (40%)
  starting transfers between devices  30.4 us (29%)
  waiting for transfers between devices  29.8 us (29%)
    ppermute x22, starting transfers between devices, exchange(): return lax.ppermute(x, 'blk', pairs)  30.4 us
    ppermute x22, waiting for transfers between devices, exchange(): return lax.ppermute(x, 'blk', pairs)  29.8 us
    pallas_call x7, Pallas kernels, attend_piece(): pl.pallas_call(functools.partial(piece_kernel, blocks > 0, len(pieces)),...  28.8 us
    pallas_call x1, Pallas kernels, attend_last(): pl.pallas_call(functools.partial(last_kernel, len(pieces), len(olds)), ou...  5.54 us
    pallas_call x1, Pallas kernels, per_device(): pl.pallas_call(prepare_kernel, out_shape=jax.ShapeDtypeStruct((SLOTS + CO...  3.89 us
  transfers between devices with their start and end apart: 22, of which 9 were waited for; matrix products, arithmetic and copies ran while one was open for 0% of the time, Pallas kernels for 34%

profile of v1, /device:TPU:4, one launch (start us, length us, event | category | flops | bytes accessed | tf_op | source)
XLA Modules:
  0.0 103.7 jit_solution(1098395685209090633)
XLA Ops:
  0.0 0.9 join.1.refs_3_
  0.9 2.0 %collective-permute-start = (bf16[128,512]{1,0:T(8,128)(2,1)S(1)}, bf16[128,512]{1,0:T(8,128)(2,1)S(1)}, u32[]{:S(2)}, u32[]{:S(2)}) collective-permute-start(bf16[128,512]{1,0:T(8,128)(2,1)S(1)} %join.1.refs_3_), channel_id=1, source_target_pairs={{0,4},{1,5},{2,6},{3,7},{4,0},{5,1},{6,2},{7,3},{8,12},{9,13},{10,... | collective-permute-start | bytes 393224 | tf_op jit(solution)/shard_map/ppermute | solution.py:414
  2.9 4.9 %collective-permute-start.1 = (bf16[128,512]{1,0:T(8,128)(2,1)S(1)}, bf16[128,512]{1,0:T(8,128)(2,1)S(1)}, u32[]{:S(2)}, u32[]{:S(2)}) collective-permute-start(bf16[128,512]{1,0:T(8,128)(2,1)S(1)} %join.1.refs_3_), channel_id=1, source_target_pairs={{0,28},{1,29},{2,30},{3,31},{4,8},{5,9},{6,10},{7,11},{8,4},{9,5},... | collective-permute-start | bytes 393224 | tf_op jit(solution)/shard_map/ppermute | solution.py:414
  8.5 0.0 copy-start.1
  8.5 0.7 copy-done.1
  9.2 3.9 %prepare.1 = bf16[144,512]{1,0:T(8,128)(2,1)S(1)} custom-call(s32[1]{0:T(128)S(6)} %copy.21.len_ref.refs_0_, s32[1,2,16]{2,1,0:T(2,128)S(1)} %copy-done.1, bf16[1,2,16,3584]{3,2,1,0:T(8,128)(2,1)} %refs_0_.2, bf16[3584,256]{1,0:T(8,128)(2,1)} %refs_1_.2, bf16[3584,256]{1,0:T(8,128)(2,1)} %refs_2_.1, bf16[128,256]{1,0:T(8,128)(2,1)} %refs_3_.1, ...), custom_call_target="tpu_custom_call" | custom-call | flops 268435456 | bytes 12582912 | tf_op jit(solution)/shard_map/prepare/pallas_call | solution.py:469
  13.1 0.0 copy-start
  13.1 0.0 copy-start.2
  13.1 0.0 collective-permute-done.refs_0_
  13.1 0.0 collective-permute-done.1.refs_1_
  13.2 1.7 %collective-permute-start.2 = (bf16[144,512]{1,0:T(8,128)(2,1)S(1)}, bf16[144,512]{1,0:T(8,128)(2,1)S(1)}, u32[]{:S(2)}, u32[]{:S(2)}) collective-permute-start(bf16[144,512]{1,0:T(8,128)(2,1)S(1)} %prepare.1), channel_id=1, source_target_pairs={{0,1},{1,0},{2,3},{3,2},{4,5},{5,4},{6,7},{7,6},{8,9},{9,8},{10,11... | collective-permute-start | bytes 442376 | tf_op jit(solution)/shard_map/ppermute | solution.py:414
  14.8 2.2 %collective-permute-start.3 = (bf16[144,512]{1,0:T(8,128)(2,1)S(1)}, bf16[144,512]{1,0:T(8,128)(2,1)S(1)}, u32[]{:S(2)}, u32[]{:S(2)}) collective-permute-start(bf16[144,512]{1,0:T(8,128)(2,1)S(1)} %prepare.1), channel_id=1, source_target_pairs={{0,3},{1,2},{2,1},{3,0},{4,7},{5,6},{6,5},{7,4},{8,11},{9,10},{10,... | collective-permute-start | bytes 442376 | tf_op jit(solution)/shard_map/ppermute | solution.py:414
  17.0 0.7 collective-permute-start.4
  17.7 0.0 collective-permute-start.7
  17.7 2.0 %collective-permute-start.8 = (bf16[128,512]{1,0:T(8,128)(2,1)S(1)}, bf16[128,512]{1,0:T(8,128)(2,1)S(1)}, u32[]{:S(2)}, u32[]{:S(2)}) collective-permute-start(bf16[128,512]{1,0:T(8,128)(2,1)S(1)} %collective-permute-done.refs_0_), channel_id=1, source_target_pairs={{0,28},{1,29},{2,30},{3,31},{4,8},{5,9},{6,10},{7,11},{8,4},{9,5},... | collective-permute-start | bytes 393224 | tf_op jit(solution)/shard_map/ppermute | solution.py:414
  19.8 2.9 %collective-permute-done.7.refs_2_ = bf16[128,512]{1,0:T(8,128)(2,1)S(1)} collective-permute-done((bf16[128,512]{1,0:T(8,128)(2,1)S(1)}, bf16[128,512]{1,0:T(8,128)(2,1)S(1)}, u32[]{:S(2)}, u32[]{:S(2)}) %collective-permute-start.7) | collective-permute-done | bytes 131104 | tf_op jit(solution)/shard_map/ppermute | solution.py:414
  22.7 0.9 collective-permute-start.12
  23.6 0.3 collective-permute-done.8.refs_3_
  23.9 2.1 %collective-permute-start.11 = (bf16[128,512]{1,0:T(8,128)(2,1)S(1)}, bf16[128,512]{1,0:T(8,128)(2,1)S(1)}, u32[]{:S(2)}, u32[]{:S(2)}) collective-permute-start(bf16[128,512]{1,0:T(8,128)(2,1)S(1)} %collective-permute-done.8.refs_3_), channel_id=1, source_target_pairs={{0,4},{1,5},{2,6},{3,7},{4,0},{5,1},{6,2},{7,3},{8,12},{9,13},{10,... | collective-permute-start | bytes 393224 | tf_op jit(solution)/shard_map/ppermute | solution.py:414
  26.0 0.0 collective-permute-done.2
  26.1 0.0 collective-permute-done.3
  26.1 0.0 collective-permute-done.4
  26.1 0.1 collective-permute-start.5
  26.2 3.2 %collective-permute-start.6 = (bf16[576,512]{1,0:T(8,128)(2,1)S(1)}, bf16[576,512]{1,0:T(8,128)(2,1)S(1)}, u32[]{:S(2)}, u32[]{:S(2)}) collective-permute-start(bf16[576,512]{1,0:T(8,128)(2,1)S(1)} %constant_dynamic-update-slice_fusion), channel_id=1, source_target_pairs={{0,28},{1,29},{2,30},{3,31},{4,8},{5,9},{6,10},{7,11},{8,4},{9,5},... | collective-permute-start | bytes 1769480 | tf_op jit(solution)/shard_map/ppermute | solution.py:414
  29.4 0.9 collective-permute-done.12.refs_5_
  30.3 0.0 collective-permute-start.13
  30.3 0.1 collective-permute-done.11.refs_4_
  30.5 12.2 %collective-permute-done.13.refs_6_ = bf16[128,512]{1,0:T(8,128)(2,1)S(1)} collective-permute-done((bf16[128,512]{1,0:T(8,128)(2,1)S(1)}, bf16[128,512]{1,0:T(8,128)(2,1)S(1)}, u32[]{:S(2)}, u32[]{:S(2)}) %collective-permute-start.13) | collective-permute-done | bytes 131104 | tf_op jit(solution)/shard_map/ppermute | solution.py:414
  42.6 0.7 collective-permute-start.16
  43.3 2.3 %collective-permute-start.17 = (bf16[1024,512]{1,0:T(8,128)(2,1)S(1)}, bf16[1024,512]{1,0:T(8,128)(2,1)S(1)}, u32[]{:S(2)}, u32[]{:S(2)}) collective-permute-start(bf16[1024,512]{1,0:T(8,128)(2,1)S(1)} %constant_dynamic-update-slice_fusion.4), channel_id=1, source_target_pairs={{0,3},{1,2},{2,1},{3,0},{4,7},{5,6},{6,5},{7,4},{8,11},{9,10},{10,... | collective-permute-start | bytes 3145736 | tf_op jit(solution)/shard_map/ppermute | solution.py:414
  45.7 0.0 copy-done
  45.7 0.0 copy-done.2
  45.7 0.6 queries.1.q_ref.refs_0_.refs_2_
  46.2 1.9 %attend_first.1 = (f32[1568,256]{1,0:T(8,128)S(1)}, f32[1568,128]{1,0:T(8,128)S(1)}) custom-call(bf16[1568,128]{1,0:T(8,128)(2,1)S(1)} %queries.1.q_ref.refs_0_.refs_2_, bf16[128,512]{1,0:T(8,128)(2,1)S(1)} %collective-permute-done.refs_0_, bf16[128,512]{1,0:T(8,128)(2,1)S(1)} %collective-permute-done.1.refs_1_, ...), custom_call_target="tpu_custom_call" | custom-call | flops 1438646272 | bytes 524288 | tf_op jit(solution)/shard_map/attend_first/pallas_call | solution.py:282
  48.2 0.0 collective-permute-done.5
  48.2 0.0 collective-permute-done.6
  48.2 2.0 %collective-permute-start.10 = (bf16[576,512]{1,0:T(8,128)(2,1)S(1)}, bf16[576,512]{1,0:T(8,128)(2,1)S(1)}, u32[]{:S(2)}, u32[]{:S(2)}) collective-permute-start(bf16[576,512]{1,0:T(8,128)(2,1)S(1)} %collective-permute-done.5), channel_id=1, source_target_pairs={{0,28},{1,29},{2,30},{3,31},{4,8},{5,9},{6,10},{7,11},{8,4},{9,5},... | collective-permute-start | bytes 1769480 | tf_op jit(solution)/shard_map/ppermute | solution.py:414
  50.2 0.0 collective-permute-start.9
  50.2 2.7 %attend_mixed.1 = (f32[1568,256]{1,0:T(8,128)S(1)}, f32[1568,128]{1,0:T(8,128)S(1)}, bf16[4,16,512]{2,1,0:T(8,128)(2,1)S(1)}, bf16[4,16,512]{2,1,0:T(8,128)(2,1)S(1)}) custom-call(bf16[1568,128]{1,0:T(8,128)(2,1)S(1)} %queries.1.q_ref.refs_0_.refs_2_, f32[1568,256]{1,0:T(8,128)S(1)} %get-tuple-element.55.refs_1_, f32[1568,128]{1,0:T(8,128)S(1)} %get-tuple-element.56.refs_2_, ...), custom_call_target="tpu_custom_call" | custom-call | flops 2697461760 | bytes 983040 | tf_op jit(solution)/shard_map/attend_mixed/pallas_call | solution.py:300
  52.9 8.9 %collective-permute-done.10 = bf16[576,512]{1,0:T(8,128)(2,1)S(1)} collective-permute-done((bf16[576,512]{1,0:T(8,128)(2,1)S(1)}, bf16[576,512]{1,0:T(8,128)(2,1)S(1)}, u32[]{:S(2)}, u32[]{:S(2)}) %collective-permute-start.10) | collective-permute-done | bytes 589856 | tf_op jit(solution)/shard_map/ppermute | solution.py:414
  61.8 0.1 collective-permute-done.9
  61.8 0.0 collective-permute-start.14
  61.8 3.4 %collective-permute-start.15 = (bf16[576,512]{1,0:T(8,128)(2,1)S(1)}, bf16[576,512]{1,0:T(8,128)(2,1)S(1)}, u32[]{:S(2)}, u32[]{:S(2)}) collective-permute-start(bf16[576,512]{1,0:T(8,128)(2,1)S(1)} %collective-permute-done.9), channel_id=1, source_target_pairs={{0,28},{1,29},{2,30},{3,31},{4,8},{5,9},{6,10},{7,11},{8,4},{9,5},... | collective-permute-start | bytes 1769480 | tf_op jit(solution)/shard_map/ppermute | solution.py:414
  65.2 2.7 %attend_span1.1 = (f32[1568,256]{1,0:T(8,128)S(1)}, f32[1568,128]{1,0:T(8,128)S(1)}, bf16[8,16,512]{2,1,0:T(8,128)(2,1)S(1)}, bf16[8,16,512]{2,1,0:T(8,128)(2,1)S(1)}) custom-call(bf16[1568,128]{1,0:T(8,128)(2,1)S(1)} %queries.1.q_ref.refs_0_.refs_2_, f32[1568,256]{1,0:T(8,128)S(1)} %get-tuple-element.61.refs_1_, f32[1568,128]{1,0:T(8,128)S(1)} %get-tuple-element.62.refs_2_, ...), custom_call_target="tpu_custom_call" | custom-call | flops 2517630976 | bytes 917504 | tf_op jit(solution)/shard_map/attend_span1/pallas_call | solution.py:300
  68.0 0.0 collective-permute-done.16.refs_3_
  68.0 0.0 collective-permute-done.17.refs_3_
  68.0 0.8 collective-permute-start.18
  68.8 1.0 collective-permute-start.19
  69.8 2.7 %attend_ctx1.1 = (f32[1568,256]{1,0:T(8,128)S(1)}, f32[1568,128]{1,0:T(8,128)S(1)}) custom-call(bf16[1568,128]{1,0:T(8,128)(2,1)S(1)} %queries.1.q_ref.refs_0_.refs_2_, f32[1568,256]{1,0:T(8,128)S(1)} %get-tuple-element.65.refs_1_, f32[1568,128]{1,0:T(8,128)S(1)} %get-tuple-element.66.refs_2_, bf16[1024,512]{1,0:T(8,128)(2,1)S(1)} %collective-permute-done.16.refs_3_), custom_call_target="tpu_custom_call" | custom-call | flops 2877292544 | bytes 1048576 | tf_op jit(solution)/shard_map/attend_ctx1/pallas_call | solution.py:300
  72.5 12.4 %attend_ctx2.1 = (f32[1568,256]{1,0:T(8,128)S(1)}, f32[1568,128]{1,0:T(8,128)S(1)}) custom-call(bf16[1568,128]{1,0:T(8,128)(2,1)S(1)} %queries.1.q_ref.refs_0_.refs_2_, f32[1568,256]{1,0:T(8,128)S(1)} %get-tuple-element.68.refs_1_, f32[1568,128]{1,0:T(8,128)S(1)} %get-tuple-element.69.refs_2_, bf16[1024,512]{1,0:T(8,128)(2,1)S(1)} %collective-permute-done.17.refs_3_), custom_call_target="tpu_custom_call" | custom-call | flops 2877292544 | bytes 1048576 | tf_op jit(solution)/shard_map/attend_ctx2/pallas_call | solution.py:300
  85.0 2.8 %attend_span2.1 = (f32[1568,256]{1,0:T(8,128)S(1)}, f32[1568,128]{1,0:T(8,128)S(1)}, bf16[8,16,512]{2,1,0:T(8,128)(2,1)S(1)}, bf16[8,16,512]{2,1,0:T(8,128)(2,1)S(1)}) custom-call(bf16[1568,128]{1,0:T(8,128)(2,1)S(1)} %queries.1.q_ref.refs_0_.refs_2_, f32[1568,256]{1,0:T(8,128)S(1)} %get-tuple-element.71.refs_1_, f32[1568,128]{1,0:T(8,128)S(1)} %get-tuple-element.72.refs_2_, ...), custom_call_target="tpu_custom_call" | custom-call | flops 2517630976 | bytes 917504 | tf_op jit(solution)/shard_map/attend_span2/pallas_call | solution.py:300
  87.8 0.0 collective-permute-done.14
  87.8 0.0 collective-permute-done.15
  87.8 0.1 collective-permute-start.20
  87.9 0.3 collective-permute-start.21
  88.3 0.0 collective-permute-done.18.refs_3_
  88.3 0.0 collective-permute-done.19.refs_4_
  88.3 2.7 %attend_ctx3.1 = (f32[1568,256]{1,0:T(8,128)S(1)}, f32[1568,128]{1,0:T(8,128)S(1)}) custom-call(bf16[1568,128]{1,0:T(8,128)(2,1)S(1)} %queries.1.q_ref.refs_0_.refs_2_, f32[1568,256]{1,0:T(8,128)S(1)} %get-tuple-element.75.refs_1_, f32[1568,128]{1,0:T(8,128)S(1)} %get-tuple-element.76.refs_2_, bf16[512,512]{1,0:T(8,128)(2,1)S(1)} %collective-permute-done.18.refs_3_, ...), custom_call_target="tpu_custom_call" | custom-call | flops 2877292544 | bytes 1048576 | tf_op jit(solution)/shard_map/attend_ctx3/pallas_call | solution.py:300
  91.0 2.8 %attend_span3.1 = (f32[1568,256]{1,0:T(8,128)S(1)}, f32[1568,128]{1,0:T(8,128)S(1)}, bf16[8,16,512]{2,1,0:T(8,128)(2,1)S(1)}, bf16[8,16,512]{2,1,0:T(8,128)(2,1)S(1)}) custom-call(bf16[1568,128]{1,0:T(8,128)(2,1)S(1)} %queries.1.q_ref.refs_0_.refs_2_, f32[1568,256]{1,0:T(8,128)S(1)} %get-tuple-element.77.refs_1_, f32[1568,128]{1,0:T(8,128)S(1)} %get-tuple-element.78.refs_2_, ...), custom_call_target="tpu_custom_call" | custom-call | flops 2517630976 | bytes 917504 | tf_op jit(solution)/shard_map/attend_span3/pallas_call | solution.py:300
  93.7 2.9 %collective-permute-done.20 = bf16[288,512]{1,0:T(8,128)(2,1)S(1)} collective-permute-done((bf16[288,512]{1,0:T(8,128)(2,1)S(1)}, bf16[288,512]{1,0:T(8,128)(2,1)S(1)}, u32[]{:S(2)}, u32[]{:S(2)}) %collective-permute-start.20) | collective-permute-done | bytes 294944 | tf_op jit(solution)/shard_map/ppermute | solution.py:414
  96.6 1.6 %collective-permute-done.21 = bf16[288,512]{1,0:T(8,128)(2,1)S(1)} collective-permute-done((bf16[288,512]{1,0:T(8,128)(2,1)S(1)}, bf16[288,512]{1,0:T(8,128)(2,1)S(1)}, u32[]{:S(2)}, u32[]{:S(2)}) %collective-permute-start.21) | collective-permute-done | bytes 294944 | tf_op jit(solution)/shard_map/ppermute | solution.py:414
  98.2 5.5 %attend_last.1 = bf16[2,128,1792]{2,1,0:T(8,128)(2,1)} custom-call(s32[1]{0:T(128)S(6)} %copy.21.len_ref.refs_0_, s32[1,2,16]{2,1,0:T(2,128)S(1)} %copy-done.2, bf16[1568,128]{1,0:T(8,128)(2,1)S(1)} %queries.1.q_ref.refs_0_.refs_2_, f32[1568,256]{1,0:T(8,128)S(1)} %get-tuple-element.81.refs_3_, f32[1568,128]{1,0:T(8,128)S(1)} %get-tuple-element.82.refs_4_, ...), custom_call_target="tpu_custom_call" | custom-call | flops 4136108032 | bytes 1507328 | tf_op jit(solution)/shard_map/attend_last/pallas_call | solution.py:384
  (16 shorter events, 0.2 us)
Async XLA Ops:
  0.9 12.2 %collective-permute-start = (bf16[128,512]{1,0:T(8,128)(2,1)S(1)}, bf16[128,512]{1,0:T(8,128)(2,1)S(1)}, u32[]{:S(2)}, u32[]{:S(2)}) collective-permute-start(bf16[128,512]{1,0:T(8,128)(2,1)S(1)} %join.1.refs_3_), channel_id=1, source_target_pairs={{0,4},{1,5},{2,6},{3,7},{4,0},{5,1},{6,2},{7,3},{8,12},{9,13},{10,... | collective-permute-start | bytes 393224 | tf_op jit(solution)/shard_map/ppermute | solution.py:414
  2.9 10.2 %collective-permute-start.1 = (bf16[128,512]{1,0:T(8,128)(2,1)S(1)}, bf16[128,512]{1,0:T(8,128)(2,1)S(1)}, u32[]{:S(2)}, u32[]{:S(2)}) collective-permute-start(bf16[128,512]{1,0:T(8,128)(2,1)S(1)} %join.1.refs_3_), channel_id=1, source_target_pairs={{0,28},{1,29},{2,30},{3,31},{4,8},{5,9},{6,10},{7,11},{8,4},{9,5},... | collective-permute-start | bytes 393224 | tf_op jit(solution)/shard_map/ppermute | solution.py:414
  8.5 0.7 copy-start.1
  13.1 32.6 %copy-start = (bf16[128,1792]{1,0:T(8,128)(2,1)S(1)}, bf16[128,1792]{1,0:T(8,128)(2,1)}, u32[]{:S(2)}) copy-start(bf16[128,1792]{1,0:T(8,128)(2,1)} %mq_ref.1) | copy-start | bytes 1376260
  13.1 32.6 %copy-start.2 = (s32[1,2,16]{2,1,0:T(2,128)S(1)}, s32[1,2,16]{2,1,0:T(2,128)}, u32[]{:S(2)}) copy-start(s32[1,2,16]{2,1,0:T(2,128)} %refs_1_.3) | copy-start | bytes 388
  13.2 12.9 %collective-permute-start.2 = (bf16[144,512]{1,0:T(8,128)(2,1)S(1)}, bf16[144,512]{1,0:T(8,128)(2,1)S(1)}, u32[]{:S(2)}, u32[]{:S(2)}) collective-permute-start(bf16[144,512]{1,0:T(8,128)(2,1)S(1)} %prepare.1), channel_id=1, source_target_pairs={{0,1},{1,0},{2,3},{3,2},{4,5},{5,4},{6,7},{7,6},{8,9},{9,8},{10,11... | collective-permute-start | bytes 442376 | tf_op jit(solution)/shard_map/ppermute | solution.py:414
  14.8 11.2 %collective-permute-start.3 = (bf16[144,512]{1,0:T(8,128)(2,1)S(1)}, bf16[144,512]{1,0:T(8,128)(2,1)S(1)}, u32[]{:S(2)}, u32[]{:S(2)}) collective-permute-start(bf16[144,512]{1,0:T(8,128)(2,1)S(1)} %prepare.1), channel_id=1, source_target_pairs={{0,3},{1,2},{2,1},{3,0},{4,7},{5,6},{6,5},{7,4},{8,11},{9,10},{10,... | collective-permute-start | bytes 442376 | tf_op jit(solution)/shard_map/ppermute | solution.py:414
  17.0 9.1 %collective-permute-start.4 = (bf16[144,512]{1,0:T(8,128)(2,1)S(1)}, bf16[144,512]{1,0:T(8,128)(2,1)S(1)}, u32[]{:S(2)}, u32[]{:S(2)}) collective-permute-start(bf16[144,512]{1,0:T(8,128)(2,1)S(1)} %prepare.1), channel_id=1, source_target_pairs={{0,2},{1,3},{2,0},{3,1},{4,6},{5,7},{6,4},{7,5},{8,10},{9,11},{10,... | collective-permute-start | bytes 442376 | tf_op jit(solution)/shard_map/ppermute | solution.py:414
  17.7 5.0 %collective-permute-start.7 = (bf16[128,512]{1,0:T(8,128)(2,1)S(1)}, bf16[128,512]{1,0:T(8,128)(2,1)S(1)}, u32[]{:S(2)}, u32[]{:S(2)}) collective-permute-start(bf16[128,512]{1,0:T(8,128)(2,1)S(1)} %collective-permute-done.1.refs_1_), channel_id=1, source_target_pairs={{0,4},{1,5},{2,6},{3,7},{4,0},{5,1},{6,2},{7,3},{8,12},{9,13},{10,... | collective-permute-start | bytes 393224 | tf_op jit(solution)/shard_map/ppermute | solution.py:414
  17.7 6.2 %collective-permute-start.8 = (bf16[128,512]{1,0:T(8,128)(2,1)S(1)}, bf16[128,512]{1,0:T(8,128)(2,1)S(1)}, u32[]{:S(2)}, u32[]{:S(2)}) collective-permute-start(bf16[128,512]{1,0:T(8,128)(2,1)S(1)} %collective-permute-done.refs_0_), channel_id=1, source_target_pairs={{0,28},{1,29},{2,30},{3,31},{4,8},{5,9},{6,10},{7,11},{8,4},{9,5},... | collective-permute-start | bytes 393224 | tf_op jit(solution)/shard_map/ppermute | solution.py:414
  22.7 7.6 %collective-permute-start.12 = (bf16[128,512]{1,0:T(8,128)(2,1)S(1)}, bf16[128,512]{1,0:T(8,128)(2,1)S(1)}, u32[]{:S(2)}, u32[]{:S(2)}) collective-permute-start(bf16[128,512]{1,0:T(8,128)(2,1)S(1)} %collective-permute-done.7.refs_2_), channel_id=1, source_target_pairs={{0,28},{1,29},{2,30},{3,31},{4,8},{5,9},{6,10},{7,11},{8,4},{9,5},... | collective-permute-start | bytes 393224 | tf_op jit(solution)/shard_map/ppermute | solution.py:414
  23.9 6.5 %collective-permute-start.11 = (bf16[128,512]{1,0:T(8,128)(2,1)S(1)}, bf16[128,512]{1,0:T(8,128)(2,1)S(1)}, u32[]{:S(2)}, u32[]{:S(2)}) collective-permute-start(bf16[128,512]{1,0:T(8,128)(2,1)S(1)} %collective-permute-done.8.refs_3_), channel_id=1, source_target_pairs={{0,4},{1,5},{2,6},{3,7},{4,0},{5,1},{6,2},{7,3},{8,12},{9,13},{10,... | collective-permute-start | bytes 393224 | tf_op jit(solution)/shard_map/ppermute | solution.py:414
  26.1 22.1 %collective-permute-start.5 = (bf16[576,512]{1,0:T(8,128)(2,1)S(1)}, bf16[576,512]{1,0:T(8,128)(2,1)S(1)}, u32[]{:S(2)}, u32[]{:S(2)}) collective-permute-start(bf16[576,512]{1,0:T(8,128)(2,1)S(1)} %constant_dynamic-update-slice_fusion), channel_id=1, source_target_pairs={{0,4},{1,5},{2,6},{3,7},{4,0},{5,1},{6,2},{7,3},{8,12},{9,13},{10,... | collective-permute-start | bytes 1769480 | tf_op jit(solution)/shard_map/ppermute | solution.py:414
  26.2 22.0 %collective-permute-start.6 = (bf16[576,512]{1,0:T(8,128)(2,1)S(1)}, bf16[576,512]{1,0:T(8,128)(2,1)S(1)}, u32[]{:S(2)}, u32[]{:S(2)}) collective-permute-start(bf16[576,512]{1,0:T(8,128)(2,1)S(1)} %constant_dynamic-update-slice_fusion), channel_id=1, source_target_pairs={{0,28},{1,29},{2,30},{3,31},{4,8},{5,9},{6,10},{7,11},{8,4},{9,5},... | collective-permute-start | bytes 1769480 | tf_op jit(solution)/shard_map/ppermute | solution.py:414
  30.3 12.3 %collective-permute-start.13 = (bf16[128,512]{1,0:T(8,128)(2,1)S(1)}, bf16[128,512]{1,0:T(8,128)(2,1)S(1)}, u32[]{:S(2)}, u32[]{:S(2)}) collective-permute-start(bf16[128,512]{1,0:T(8,128)(2,1)S(1)} %collective-permute-done.12.refs_5_), channel_id=1, source_target_pairs={{0,4},{1,5},{2,6},{3,7},{4,0},{5,1},{6,2},{7,3},{8,12},{9,13},{10,... | collective-permute-start | bytes 393224 | tf_op jit(solution)/shard_map/ppermute | solution.py:414
  42.6 25.3 %collective-permute-start.16 = (bf16[1024,512]{1,0:T(8,128)(2,1)S(1)}, bf16[1024,512]{1,0:T(8,128)(2,1)S(1)}, u32[]{:S(2)}, u32[]{:S(2)}) collective-permute-start(bf16[1024,512]{1,0:T(8,128)(2,1)S(1)} %constant_dynamic-update-slice_fusion.4), channel_id=1, source_target_pairs={{0,1},{1,0},{2,3},{3,2},{4,5},{5,4},{6,7},{7,6},{8,9},{9,8},{10,11... | collective-permute-start | bytes 3145736 | tf_op jit(solution)/shard_map/ppermute | solution.py:414
  43.3 24.6 %collective-permute-start.17 = (bf16[1024,512]{1,0:T(8,128)(2,1)S(1)}, bf16[1024,512]{1,0:T(8,128)(2,1)S(1)}, u32[]{:S(2)}, u32[]{:S(2)}) collective-permute-start(bf16[1024,512]{1,0:T(8,128)(2,1)S(1)} %constant_dynamic-update-slice_fusion.4), channel_id=1, source_target_pairs={{0,3},{1,2},{2,1},{3,0},{4,7},{5,6},{6,5},{7,4},{8,11},{9,10},{10,... | collective-permute-start | bytes 3145736 | tf_op jit(solution)/shard_map/ppermute | solution.py:414
  48.2 13.6 %collective-permute-start.10 = (bf16[576,512]{1,0:T(8,128)(2,1)S(1)}, bf16[576,512]{1,0:T(8,128)(2,1)S(1)}, u32[]{:S(2)}, u32[]{:S(2)}) collective-permute-start(bf16[576,512]{1,0:T(8,128)(2,1)S(1)} %collective-permute-done.5), channel_id=1, source_target_pairs={{0,28},{1,29},{2,30},{3,31},{4,8},{5,9},{6,10},{7,11},{8,4},{9,5},... | collective-permute-start | bytes 1769480 | tf_op jit(solution)/shard_map/ppermute | solution.py:414
  50.2 11.7 %collective-permute-start.9 = (bf16[576,512]{1,0:T(8,128)(2,1)S(1)}, bf16[576,512]{1,0:T(8,128)(2,1)S(1)}, u32[]{:S(2)}, u32[]{:S(2)}) collective-permute-start(bf16[576,512]{1,0:T(8,128)(2,1)S(1)} %collective-permute-done.6), channel_id=1, source_target_pairs={{0,4},{1,5},{2,6},{3,7},{4,0},{5,1},{6,2},{7,3},{8,12},{9,13},{10,... | collective-permute-start | bytes 1769480 | tf_op jit(solution)/shard_map/ppermute | solution.py:414
  61.8 25.9 %collective-permute-start.14 = (bf16[576,512]{1,0:T(8,128)(2,1)S(1)}, bf16[576,512]{1,0:T(8,128)(2,1)S(1)}, u32[]{:S(2)}, u32[]{:S(2)}) collective-permute-start(bf16[576,512]{1,0:T(8,128)(2,1)S(1)} %collective-permute-done.10), channel_id=1, source_target_pairs={{0,4},{1,5},{2,6},{3,7},{4,0},{5,1},{6,2},{7,3},{8,12},{9,13},{10,... | collective-permute-start | bytes 1769480 | tf_op jit(solution)/shard_map/ppermute | solution.py:414
  61.8 25.9 %collective-permute-start.15 = (bf16[576,512]{1,0:T(8,128)(2,1)S(1)}, bf16[576,512]{1,0:T(8,128)(2,1)S(1)}, u32[]{:S(2)}, u32[]{:S(2)}) collective-permute-start(bf16[576,512]{1,0:T(8,128)(2,1)S(1)} %collective-permute-done.9), channel_id=1, source_target_pairs={{0,28},{1,29},{2,30},{3,31},{4,8},{5,9},{6,10},{7,11},{8,4},{9,5},... | collective-permute-start | bytes 1769480 | tf_op jit(solution)/shard_map/ppermute | solution.py:414
  68.0 20.2 %collective-permute-start.18 = (bf16[512,512]{1,0:T(8,128)(2,1)S(1)}, bf16[512,512]{1,0:T(8,128)(2,1)S(1)}, u32[]{:S(2)}, u32[]{:S(2)}) collective-permute-start(bf16[512,512]{1,0:T(8,128)(2,1)S(1)} %slice.12), channel_id=1, source_target_pairs={{0,1},{1,0},{2,3},{3,2},{4,5},{5,4},{6,7},{7,6},{8,9},{9,8},{10,11... | collective-permute-start | bytes 1572872 | tf_op jit(solution)/shard_map/ppermute | solution.py:414
  68.8 19.4 %collective-permute-start.19 = (bf16[512,512]{1,0:T(8,128)(2,1)S(1)}, bf16[512,512]{1,0:T(8,128)(2,1)S(1)}, u32[]{:S(2)}, u32[]{:S(2)}) collective-permute-start(bf16[512,512]{1,0:T(8,128)(2,1)S(1)} %slice.13), channel_id=1, source_target_pairs={{0,3},{1,2},{2,1},{3,0},{4,7},{5,6},{6,5},{7,4},{8,11},{9,10},{10,... | collective-permute-start | bytes 1572872 | tf_op jit(solution)/shard_map/ppermute | solution.py:414
  87.8 8.8 %collective-permute-start.20 = (bf16[288,512]{1,0:T(8,128)(2,1)S(1)}, bf16[288,512]{1,0:T(8,128)(2,1)S(1)}, u32[]{:S(2)}, u32[]{:S(2)}) collective-permute-start(bf16[288,512]{1,0:T(8,128)(2,1)S(1)} %slice.14), channel_id=1, source_target_pairs={{0,4},{1,5},{2,6},{3,7},{4,0},{5,1},{6,2},{7,3},{8,12},{9,13},{10,... | collective-permute-start | bytes 884744 | tf_op jit(solution)/shard_map/ppermute | solution.py:414
  87.9 10.3 %collective-permute-start.21 = (bf16[288,512]{1,0:T(8,128)(2,1)S(1)}, bf16[288,512]{1,0:T(8,128)(2,1)S(1)}, u32[]{:S(2)}, u32[]{:S(2)}) collective-permute-start(bf16[288,512]{1,0:T(8,128)(2,1)S(1)} %slice.15), channel_id=1, source_target_pairs={{0,28},{1,29},{2,30},{3,31},{4,8},{5,9},{6,10},{7,11},{8,4},{9,5},... | collective-permute-start | bytes 884744 | tf_op jit(solution)/shard_map/ppermute | solution.py:414
